TPU v7x, 512 devices: a whole 4x4x16 slice. The times are simulated.
512 devices in a mesh: basis: 16 (over x, y), docs: 32 (over z, core).
Axes of the slice: x: 4, y: 4, z: 16, core: 2. Of those that a mesh axis runs over, the one named last changes fastest.
Arguments:
- eig_in: bfloat16 [28672, 28672], P('basis', 'docs'), may hold values from -0.03125 to 0.03125
- eig_out: bfloat16 [8192, 8192], P('basis', 'docs'), may hold values from -0.0625 to 0.0625
- eigvals: bfloat16 [8192, 28672], P('basis', 'docs'), may hold values from 0.0025 to 3.6
- out_factors: bfloat16 [8192, 256], P('docs'), may hold values from -1.1953125 to 1.1953125
- in_factors: bfloat16 [28672, 256], P(('basis', 'docs')), may hold values from -1.1953125 to 1.1953125
- test_matrix: bfloat16 [28672, 32], P('docs'), may hold values from -0.03125 to 0.03125
- activations: bfloat16 [4096, 28672], P('docs', 'basis'), may hold values from -6 to 6
- gradients: bfloat16 [4096, 8192], P('docs', 'basis'), may hold values from -0.00059890747 to 0.00059890747
- doc_lengths: int32 [128], replicated, may hold values from 1 to 96, 4096 in all
Outputs:
- scores: float32 [4096, 4], P('docs')
- doc_influence: float32 [128, 4], replicated
Inputs may be any that keep to these rules, and one draw needn't show every extreme that they name: `doc_lengths`: the documents lie end to end in token order and their lengths sum to 4096.
All inputs are finite; a program needn't handle non-finite values.
Results may differ from a plain program's by a relative error of at most 0.0085.
Values may be sent and summed in bfloat16 or wider, within the bound.
A program may use at most 64 MiB of HBM per device.

v0:
```python
import jax
import jax.numpy as jnp
from jax import lax
from jax.sharding import PartitionSpec as P

QUERIES = 4
LQ = 64
RANK = 32


damping = 0.1
highest = lax.Precision.HIGHEST


def local(
    eig_in,
    eig_out,
    eigvals,
    out_factors,
    in_factors,
    test_matrix,
    activations,
    gradients,
    doc_lengths,
):
    cols_in = eig_in.shape[1]
    rows_out = eig_out.shape[0]
    cols_out = eig_out.shape[1]
    tok_count = activations.shape[0]
    partial_in = lax.dot_general(
        eig_in,
        lax.all_gather(in_factors, "docs", axis=0, tiled=True),
        (((0,), (0,)), ((), ())),
        preferred_element_type=jnp.float32,
    )
    partial_out = jnp.dot(eig_out, out_factors, preferred_element_type=jnp.float32)
    rot_in = lax.psum(partial_in, "basis").astype(jnp.bfloat16)
    rot_out = lax.psum(partial_out, "docs").astype(jnp.bfloat16)
    weight = 1.0 / (eigvals.astype(jnp.float32) + damping)
    moment = (
        jnp.einsum(
            "iqs,jqs->qij",
            rot_out.reshape(rows_out, QUERIES, LQ),
            rot_in.reshape(cols_in, QUERIES, LQ),
            preferred_element_type=jnp.float32,
        )
        * weight[None]
    )
    sketch_part = jnp.einsum(
        "jr,qij->qri", test_matrix.astype(jnp.float32), moment, precision=highest
    )
    sketch = lax.psum(sketch_part, "docs")
    eig_wide = eig_out.astype(jnp.float32)
    gram_part = jnp.einsum("qri,qsi->qrs", sketch, sketch, precision=highest)
    gram_sum = lax.psum(gram_part, "basis")
    lower_factor = jnp.linalg.cholesky(gram_sum)
    range_rows = lax.linalg.triangular_solve(lower_factor, sketch, left_side=True, lower=True)
    proj_part = jnp.einsum("qri,qij->qrj", range_rows, moment, precision=highest)
    left_part = jnp.einsum("ia,qri->aqr", eig_wide, range_rows, precision=highest)
    projected, left_total = lax.psum((proj_part, left_part), "basis")
    left_sum = left_total.reshape(cols_out, QUERIES * RANK)
    projected_low = projected.astype(jnp.bfloat16).reshape(QUERIES * RANK, cols_in)
    right_part = lax.dot_general(
        eig_in, projected_low, (((1,), (1,)), ((), ())), preferred_element_type=jnp.float32
    )
    right_factor = lax.psum(right_part, "docs").astype(jnp.bfloat16)
    left_block = left_sum.astype(jnp.bfloat16)
    gathered = lax.all_gather(left_block, "docs", axis=0, tiled=True)
    rows_here = gradients.shape[1]
    left_local = lax.dynamic_slice_in_dim(
        gathered, lax.axis_index("basis") * rows_here, rows_here, 0
    )
    token_in, token_out = lax.psum(
        (
            jnp.dot(activations, right_factor, preferred_element_type=jnp.float32),
            jnp.dot(gradients, left_local, preferred_element_type=jnp.float32),
        ),
        "basis",
    )
    scores = (token_in * token_out).reshape(tok_count, QUERIES, RANK).sum(axis=2)
    positions = lax.axis_index("docs") * tok_count + jnp.arange(tok_count, dtype=jnp.int32)
    doc_ends = jnp.cumsum(doc_lengths)
    doc_starts = doc_ends - doc_lengths
    member = (
        (positions[:, None] >= doc_starts[None, :]) & (positions[:, None] < doc_ends[None, :])
    ).astype(jnp.float32)
    doc_part = lax.dot_general(member, scores, (((0,), (0,)), ((), ())), precision=highest)
    doc_influence = lax.psum(doc_part, "docs")
    return (scores, doc_influence)


def solution(mesh):
    return jax.shard_map(
        local,
        mesh=mesh,
        in_specs=(
            P("basis", "docs"),
            P("basis", "docs"),
            P("basis", "docs"),
            P("docs", None),
            P(("basis", "docs"), None),
            P("docs", None),
            P("docs", "basis"),
            P("docs", "basis"),
            P(),
        ),
        out_specs=(P("docs", None), P()),
        check_vma=False,
    )
```

profile of v0, /device:TPU:1, one launch (start us, length us, event | category | flops | bytes accessed | tf_op | source)
XLA Modules:
  0.0 913.8 jit_solution(15567339814722181471)
XLA Ops:
  7.2 0.0 copy-start
  7.2 0.0 all-reduce.9.cloned.1.call-start
  7.2 40.4 %all_gather.6 = bf16[1792,256]{1,0:T(8,128)(2,1)S(1)} all-gather(bf16[56,256]{1,0:T(8,128)(2,1)} %param.13), channel_id=1, replica_groups=mesh['basis'=16,'docs'=32] {'docs'}, dimensions={0}, use_global_device_ids=true | all-gather | bytes 946176 | tf_op jit(solution)/shard_map/all_gather | solution.py:32
  47.7 0.0 copy-done
  47.7 2.0 fusion.22
  49.6 73.3 %all-reduce.12 = bf16[896,256]{1,0:T(8,128)(2,1)} all-reduce(f32[896,256]{1,0:T(8,128)} %fusion.22), channel_id=1, replica_groups=mesh['basis'=16,'docs'=32] {'basis'}, use_global_device_ids=true, to_apply=%region_1.0 | all-reduce | flops 229376 | bytes 1376256 | tf_op jit(solution)/shard_map/psum | solution.py:37
  123.0 2.0 copy.24
  125.0 0.0 copy-done.3
  125.0 1.9 fusion.21
  126.9 104.9 %all-reduce.13 = bf16[512,256]{1,0:T(8,128)(2,1)} all-reduce(f32[512,256]{1,0:T(8,128)} %fusion.21), channel_id=1, replica_groups=mesh['basis'=16,'docs'=32] {'docs'}, use_global_device_ids=true, to_apply=%region_0.0 | all-reduce | flops 131072 | bytes 786432 | tf_op jit(solution)/shard_map/psum | solution.py:38
  231.8 1.8 copy.23
  233.6 1.4 add_divide_fusion
  235.0 0.0 copy-start.4
  235.1 2.9 fusion.23
  237.9 0.0 copy-done.2
  237.9 0.0 copy-start.1
  237.9 3.0 copy-done.1
  240.9 4.8 fusion.6
  245.7 0.0 all-reduce.9.cloned.1.call-update
  245.7 0.0 all-gather.2.cloned.1.call-start
  245.8 205.3 %all-reduce.9.cloned.1.call-done = f32[4,32,512]{2,1,0:T(8,128)} async-done(((f32[4,32,512]{2,1,0:T(8,128)}), f32[4,32,512]{2,1,0:T(8,128)}) %all-reduce.9.cloned.1.call-update) | async-done | bytes 262160 | tf_op jit(solution)/shard_map/psum | solution.py:52
  451.1 2.1 fusion.24
  453.2 61.2 %psum.73 = f32[4,32,32]{1,2,0:T(8,128)S(1)} all-reduce(f32[4,32,32]{1,2,0:T(8,128)} %fusion.24), channel_id=1, replica_groups=mesh['basis'=16,'docs'=32] {'basis'}, use_global_device_ids=true, to_apply=%region_3.0 | all-reduce | flops 4096 | bytes 32768 | tf_op jit(solution)/shard_map/psum | solution.py:55
  514.4 0.7 copy.26
  515.1 1.5 fusion.14
  516.5 12.4 %custom-call.7 = f32[4,32,32]{2,1,0:T(8,128)S(1)} custom-call(f32[4,32,32]{2,1,0:T(8,128)} %fusion.14), custom_call_target="Cholesky" | custom-call | tf_op jit(solution)/shard_map/jit(cholesky)/cholesky | solution.py:56
  529.0 0.1 compare_reduce_fusion
  529.1 0.7 select_bitcast_fusion
  529.8 10.5 %custom-call.8 = f32[4,1,32,32]{2,3,1,0:T(8,128)S(1)} custom-call(f32[4,1,32,32]{3,2,1,0:T(8,128)} %select_bitcast_fusion), custom_call_target="InvertDiagBlocksLowerTriangular" | custom-call | tf_op jit(solution)/shard_map/triangular_solve | solution.py:57
  540.3 1.4 fusion.12
  541.7 7.3 fusion
  549.0 0.9 convolution_bitcast_fusion.1
  549.9 63.2 %all-reduce.14 = (bf16[4,32,896]{2,1,0:T(8,128)(2,1)S(1)}, bf16[256,4,32]{0,2,1:T(8,128)(2,1)}) all-reduce(f32[4,32,896]{2,1,0:T(8,128)} %fusion, f32[256,4,32]{0,2,1:T(8,128)} %convolution_bitcast_fusion.1), channel_id=1, replica_groups=mesh['basis'=16,'docs'=32] {'basis'}, use_global_device_ids=true, to_apply=%region_6.7 | all-reduce | flops 147456 | bytes 884736 | tf_op jit(solution)/shard_map/psum | solution.py:60
  613.1 0.0 all-gather.2.cloned.1.call-update
  613.1 0.0 all-reduce.11.cloned.1.call-start
  613.2 0.0 copy-start.6
  613.2 1.9 convolution_bitcast_fusion
  615.2 125.7 %all-reduce.15 = bf16[1792,128]{0,1:T(8,128)(2,1)} all-reduce(f32[1792,128]{0,1:T(8,128)} %convolution_bitcast_fusion), channel_id=1, replica_groups=mesh['basis'=16,'docs'=32] {'docs'}, use_global_device_ids=true, to_apply=%region_7.8 | all-reduce | flops 229376 | bytes 1376256 | tf_op jit(solution)/shard_map/psum | solution.py:66
  740.8 2.1 convolution_bitcast_fusion.3
  742.9 1.8 convolution_bitcast_fusion.2
  744.6 0.0 all-reduce.11.cloned.1.call-update
  744.7 0.1 copy.28
  744.8 0.2 reduce-window.8
  745.0 0.1 reduce.6
  745.1 111.6 %all-reduce.11.cloned.1.call-done = (f32[128,128]{0,1:T(8,128)}, f32[128,128]{0,1:T(8,128)}) async-done(((f32[128,128]{0,1:T(8,128)}, f32[128,128]{0,1:T(8,128)}), (f32[128,128]{0,1:T(8,128)}, f32[128,128]{0,1:T(8,128)})) %all-reduce.11.cloned.1.call-update) | async-done | bytes 131088 | tf_op jit(solution)/shard_map/psum | solution.py:73
  856.7 0.9 bitcast_reduce_fusion
  857.6 0.2 fusion.15
  857.8 49.5 %psum.79 = f32[128,4]{0,1:T(4,128)} all-reduce(f32[128,4]{0,1:T(4,128)S(1)} %fusion.15), channel_id=1, replica_groups=mesh['basis'=16,'docs'=32] {'docs'}, use_global_device_ids=true, to_apply=%region_13.14 | all-reduce | flops 512 | bytes 4096 | tf_op jit(solution)/shard_map/psum | solution.py:88
  (12 shorter events, 0.1 us)
Async XLA Ops:
  7.2 40.5 %copy-start = (bf16[1792,896]{1,0:T(8,128)(2,1)S(1)}, bf16[1792,896]{1,0:T(8,128)(2,1)}, u32[]{:S(2)}) copy-start(bf16[1792,896]{1,0:T(8,128)(2,1)} %param.9) | copy-start | bytes 9633796
  7.2 444.0 %all-reduce.9.cloned.1.call-start = ((), (), s32[]{:S(2)}) async-start(), calls=%async_computation | async-start | bytes 524288 | tf_op jit(solution)/shard_map/psum | solution.py:52
  47.7 77.3 %copy-start.3 = (bf16[512,256]{1,0:T(8,128)(2,1)S(1)}, bf16[512,256]{1,0:T(8,128)(2,1)}, u32[]{:S(2)}) copy-start(bf16[512,256]{1,0:T(8,128)(2,1)} %param.10) | copy-start | bytes 786436
  235.0 2.9 copy-start.2
  235.0 5.9 copy-start.4
  237.9 3.0 copy-start.1
  245.7 497.1 %all-gather.2.cloned.1.call-start = ((), (), s32[]{:S(2)}) async-start(), calls=%async_computation.1 | async-start | bytes 2162688 | tf_op jit(solution)/shard_map/all_gather | solution.py:68
  613.1 243.5 %all-reduce.11.cloned.1.call-start = ((), (), s32[]{:S(2)}) async-start(), calls=%async_computation.2 | async-start | bytes 262144 | tf_op jit(solution)/shard_map/psum | solution.py:73
  613.2 131.5 %copy-start.6 = (s32[128]{0:T(128)S(1)}, s32[128]{0:T(128)}, u32[]{:S(2)}) copy-start(s32[128]{0:T(128)} %param.17) | copy-start | bytes 1540
  857.6 49.7 %copy-start.5 = (f32[128,4]{0,1:T(4,128)}, f32[128,4]{0,1:T(4,128)S(1)}, u32[]{:S(2)}) copy-start(f32[128,4]{0,1:T(4,128)S(1)} %bitcast_reduce_fusion) | copy-start | bytes 6148
Sparse Core Ops, SparseCore 0:
  245.9 205.2 all-reduce.8
  613.3 97.2 all-gather.1
  744.8 111.8 all-reduce.10
where the time goes:
time: 915 us; the launch traced here: 914 us
  blocking collectives  518 us (57%)
  waiting for transfers between devices  317 us (35%)
  matrix products  29.2 us (3%)
  other arithmetic  27.9 us (3%)
  between operations  13.9 us (2%)
    psum x1, waiting for transfers between devices, local(): sketch = lax.psum(sketch_part, 'docs')  205 us
    psum x1, blocking collectives, local(): right_factor = lax.psum(right_part, 'docs').astype(jnp.bfloat16)  126 us
    psum x1, waiting for transfers between devices, local(): lax.psum((jnp.dot(activations, right_factor, preferred_element_type=jnp.f...  112 us
    psum x1, blocking collectives, local(): rot_out = lax.psum(partial_out, 'docs').astype(jnp.bfloat16)  105 us
    psum x1, blocking collectives, local(): rot_in = lax.psum(partial_in, 'basis').astype(jnp.bfloat16)  73.3 us
    psum x1, blocking collectives, local(): projected, left_total = lax.psum((proj_part, left_part), 'basis')  63.2 us
    psum x1, blocking collectives, local(): gram_sum = lax.psum(gram_part, 'basis')  61.2 us
    psum x1, blocking collectives, local(): doc_influence = lax.psum(doc_part, 'docs')  49.5 us
  transfers between devices with their start and end apart: 3, of which 2 were waited for; matrix products, arithmetic and copies ran while one was open for 0% of the time, Pallas kernels for 0%

commit v1 on v0

v1 whole, which is shorter than its diff:
```python
import functools

import jax
import jax.numpy as jnp
from jax import lax
from jax.experimental import pallas as pl
from jax.experimental.pallas import tpu as pltpu
from jax.sharding import PartitionSpec as P

QUERIES = 4
LQ = 64
RANK = 32
QR = QUERIES * RANK
QC = QUERIES * LQ
DAMPING = 0.1
MESH = pl.DeviceIdType.MESH
HIGHEST = lax.Precision.HIGHEST
F32 = jnp.float32
BF16 = jnp.bfloat16


def nn(a, b, precision=None):
    return lax.dot_general(a, b, (((1,), (0,)), ((), ())), precision=precision, preferred_element_type=F32)


def nt(a, b, precision=None):
    return lax.dot_general(a, b, (((1,), (1,)), ((), ())), precision=precision, preferred_element_type=F32)


def tn(a, b, precision=None):
    return lax.dot_general(a, b, (((0,), (0,)), ((), ())), precision=precision, preferred_element_type=F32)


def iota(shape, axis):
    return lax.broadcasted_iota(jnp.int32, shape, axis)


def near_first(n):
    order = []
    for k in range(1, n // 2 + 1):
        order.append(k)
        if n - k != k:
            order.append(n - k)
    return order


def wait_bytes(ref, sem):
    pltpu.make_async_copy(ref, ref, sem).wait()


def body(
    nb,
    nz,
    ein_h,
    eout_h,
    lam_h,
    of_h,
    inf_h,
    te_h,
    act_h,
    gr_h,
    len_h,
    scores_o,
    doc_o,
    ein,
    eout,
    lam,
    outf,
    te,
    act,
    gr,
    lens,
    xin,
    acc,
    wgt,
    tsel,
    mom,
    pin_s,
    pin_r,
    rin,
    po_s,
    po_p,
    po_z,
    po_r,
    ro,
    sk_s,
    sk_p,
    sk_z,
    sk_r,
    sk,
    gm_s,
    gm_r,
    pj_s,
    pj_r,
    pj,
    lf_s,
    lf_r,
    lf_c,
    lf,
    rt_s,
    rt_p,
    rt_z,
    rt_r,
    rt,
    tk_s,
    tk_r,
    sc,
    dc_s,
    dc_p,
    dc_z,
    dc_r,
    in_sem,
    a_send,
    a_recv,
    f_send,
    f_recv,
    sends,
    recvs,
):
    b = lax.axis_index("basis")
    d = lax.axis_index("docs")
    z = lax.div(d, 2)
    c = lax.rem(d, 2)
    mate = {"docs": z * 2 + (1 - c)}
    sent = []

    def zdev(k):
        return {"docs": lax.rem(z + k, nz) * 2 + c}

    def bdev(k):
        return {"basis": lax.rem(b + k, nb)}

    def put(src, dst, s, r, dev):
        pltpu.make_async_remote_copy(
            src_ref=src, dst_ref=dst, send_sem=s, recv_sem=r, device_id=dev, device_id_type=MESH
        ).start()

    def to_mate(src, dst, ch):
        put(src, dst, sends.at[ch], recvs.at[ch], mate)
        sent.append((src, sends.at[ch]))

    def scatter(n, dev, me, src, base, dst, ch):
        for k in near_first(n):
            put(
                src.at[base + lax.rem(me + k, n)],
                dst.at[k],
                sends.at[ch],
                recvs.at[ch],
                dev(k),
            )
        sent.append((dst.at[pl.ds(0, n - 1)], sends.at[ch]))

    def spread(n, dev, ref, where, ch):
        for k in near_first(n):
            put(ref.at[where], ref.at[where], sends.at[ch], recvs.at[ch], dev(k))
        sent.append((ref.at[pl.ds(0, n - 1)], sends.at[ch]))

    def arrived(n, ref, ch):
        wait_bytes(ref.at[pl.ds(0, n - 1)], recvs.at[ch])

    def added(n, first, ref):
        total = first.astype(F32)
        for k in range(1, n):
            total = total + ref[k].astype(F32)
        return total

    loads = []
    for i, (src, dst) in enumerate(
        (
            (inf_h, xin.at[d]),
            (eout_h, eout),
            (of_h, outf),
            (ein_h, ein),
            (lam_h, lam),
            (te_h, te),
            (act_h, act),
            (gr_h, gr),
            (len_h, lens),
        )
    ):
        cp = pltpu.make_async_copy(src, dst, in_sem.at[i])
        cp.start()
        loads.append(cp)

    barrier = pltpu.get_barrier_semaphore()
    for k in near_first(nz):
        pl.semaphore_signal(barrier, inc=1, device_id=zdev(k), device_id_type=MESH)
    for k in near_first(nb):
        pl.semaphore_signal(barrier, inc=1, device_id=bdev(k), device_id_type=MESH)
    pl.semaphore_signal(barrier, inc=1, device_id=mate, device_id_type=MESH)
    twin = {"basis": z, "docs": b * 2 + c}

    @pl.when(b != z)
    def _():
        pl.semaphore_signal(barrier, inc=1, device_id=twin, device_id_type=MESH)

    pl.semaphore_wait(barrier, nz + nb - 1 + jnp.where(b != z, 1, 0))

    loads[0].wait()
    for k in near_first(nz):
        put(xin.at[d], xin.at[d], a_send, a_recv.at[k], zdev(k))
    sent.append((xin.at[pl.ds(0, nz - 1)], a_send))
    put(xin.at[d], xin.at[d], f_send, f_recv.at[0], mate)

    loads[1].wait()
    loads[2].wait()
    part = nn(eout[...], outf[...])
    po_s[...] = part.astype(BF16).reshape(po_s.shape)
    to_mate(po_s.at[pl.ds((1 - c) * nz, nz)], po_p, 0)

    loads[4].wait()
    wgt[...] = 1.0 / (lam[...].astype(F32) + DAMPING)
    loads[5].wait()
    wide = jnp.concatenate([te[...].astype(F32)] * QUERIES, axis=1)
    for q in range(QUERIES):
        tsel[q] = jnp.where(lax.div(iota(wide.shape, 1), RANK) == q, wide, 0.0).astype(BF16)

    wait_bytes(po_p, recvs.at[0])
    po_z[...] = (po_s[pl.ds(c * nz, nz)].astype(F32) + po_p[...].astype(F32)).astype(BF16)

    for k in near_first(nz):
        origin = lax.rem(z - k + nz, nz) * 2 + c
        pltpu.make_async_copy(xin.at[origin], xin.at[origin], a_recv.at[k]).wait()
        put(xin.at[origin], xin.at[origin], f_send, f_recv.at[k], mate)
    sent.append((xin.at[pl.ds(0, nz)], f_send))
    scatter(nz, zdev, z, po_z, 0, po_r, 1)
    for k in range(nz):
        other = lax.rem(z - k + nz, nz) * 2 + 1 - c
        pltpu.make_async_copy(xin.at[other], xin.at[other], f_recv.at[k]).wait()

    loads[3].wait()
    pieces = xin.shape[0] // 4
    rows = pieces * xin.shape[1]
    for i in range(4):
        x = xin[pl.ds(i * pieces, pieces)].astype(F32).reshape(rows, QC).astype(BF16)
        t = tn(x, ein[pl.ds(i * rows, rows), :])
        if i == 0:
            acc[...] = t
        elif i < 3:
            acc[...] += t
        else:
            t = acc[...] + t
            pin_s[...] = t.astype(BF16).reshape(pin_s.shape)
    scatter(nb, bdev, b, pin_s, 0, pin_r, 2)

    arrived(nz, po_r, 1)
    ro[c * nz + z] = added(nz, po_z[z], po_r).astype(BF16)
    spread(nz, zdev, ro, c * nz + z, 3)

    arrived(nb, pin_r, 2)
    rin[b] = added(nb, pin_s[b], pin_r).astype(BF16)
    spread(nb, bdev, rin, b, 4)

    arrived(nz, ro, 3)
    to_mate(ro.at[pl.ds(c * nz, nz)], ro.at[pl.ds(c * nz, nz)], 5)
    wait_bytes(ro.at[pl.ds(0, nz)], recvs.at[5])
    arrived(nb, rin, 4)

    rows_out = eout.shape[0]
    cols_in = ein.shape[1]
    rotin = rin[...].reshape(QC, cols_in)
    rotout = ro[...].reshape(rows_out, QC)
    step = 128
    per = sk_s.shape[1]
    for i in range(rows_out // step):
        block = rotout[i * step : (i + 1) * step, :]
        lane = lax.div(iota(block.shape, 1), LQ)
        total = None
        for q in range(QUERIES):
            only = jnp.where(lane == q, block.astype(F32), 0.0).astype(BF16)
            m = (nn(only, rotin) * wgt[pl.ds(i * step, step), :]).astype(BF16)
            mom[q, pl.ds(i * step, step), :] = m
            t = nn(m, tsel[q])
            total = t if total is None else total + t
        sk_s[pl.ds(i * step // per, step // per)] = total.astype(BF16).reshape(step // per, per, QR)
    to_mate(sk_s.at[pl.ds((1 - c) * nz, nz)], sk_p, 6)
    wait_bytes(sk_p, recvs.at[6])
    sk_z[...] = (sk_s[pl.ds(c * nz, nz)].astype(F32) + sk_p[...].astype(F32)).astype(BF16)
    scatter(nz, zdev, z, sk_z, 0, sk_r, 7)
    arrived(nz, sk_r, 7)
    sk[c * nz + z] = added(nz, sk_z[z], sk_r).astype(BF16)
    spread(nz, zdev, sk, c * nz + z, 8)
    arrived(nz, sk, 8)
    to_mate(sk.at[pl.ds(c * nz, nz)], sk.at[pl.ds(c * nz, nz)], 9)
    wait_bytes(sk.at[pl.ds(0, nz)], recvs.at[9])

    sketch = sk[...].reshape(rows_out, QR).astype(F32).T.astype(BF16)
    gram = nt(sketch, sketch)
    lane_q = lax.div(iota((RANK, QR), 1), RANK)
    mine = jnp.zeros((RANK, QR), F32)
    for q in range(QUERIES):
        mine = mine + jnp.where(lane_q == q, gram[q * RANK : (q + 1) * RANK, :], 0.0)
    gm_s[...] = mine
    for k in near_first(nb):
        put(gm_s, gm_r.at[k], sends.at[10], recvs.at[10], bdev(k))
    sent.append((gm_r.at[pl.ds(0, nb - 1)], sends.at[10]))

    raw = jnp.concatenate(
        [nn(sketch[q * RANK : (q + 1) * RANK, :], mom[q]) for q in range(QUERIES)], axis=0
    )
    acc[pl.ds(0, QR), :] = raw
    left_raw = nn(sketch, eout[...])

    arrived(nb, gm_r, 10)
    a0 = added(nb, mine, gm_r)
    row = iota((RANK, QR), 0)
    lane = iota((RANK, QR), 1)
    in_q = lane - lane_q * RANK

    def over_lanes(x):
        out = jnp.zeros((RANK, QR), F32)
        for q in range(QUERIES):
            s = jnp.sum(jnp.where(lane_q == q, x, 0.0), axis=1, keepdims=True)
            out = jnp.where(lane_q == q, s, out)
        return out

    def eliminate(k, carry):
        a, e = carry
        col = over_lanes(jnp.where(in_q == k, a, 0.0))
        at = row == k
        pivot = jnp.sum(jnp.where(at, col, 0.0), axis=0, keepdims=True)
        row_a = jnp.sum(jnp.where(at, a, 0.0), axis=0, keepdims=True)
        row_e = jnp.sum(jnp.where(at, e, 0.0), axis=0, keepdims=True)
        f = jnp.where(row > k, col / pivot, 0.0)
        return a - f * row_a, e - f * row_e

    e0 = jnp.where(in_q == row, 1.0, 0.0).astype(F32)
    a1, e1 = lax.fori_loop(0, RANK, eliminate, (a0, e0))
    inv = e1 / jnp.sqrt(over_lanes(jnp.where(in_q == row, a1, 0.0)))
    tall = jnp.concatenate([inv] * QUERIES, axis=0)
    same = lax.div(iota((QR, QR), 0), RANK) == lax.div(iota((QR, QR), 1), RANK)
    solve = jnp.where(same, tall, 0.0)

    pj_s[...] = nn(solve, acc[pl.ds(0, QR), :], HIGHEST).reshape(pj_s.shape).astype(BF16)
    scatter(nb, bdev, b, pj_s, 0, pj_r, 11)
    lf_s[...] = nn(solve, left_raw, HIGHEST).T.reshape(lf_s.shape).astype(BF16)
    scatter(nb, bdev, b, lf_s, 0, lf_r, 12)
    arrived(nb, pj_r, 11)
    pj[b] = added(nb, pj_s[b], pj_r).astype(BF16)
    spread(nb, bdev, pj, b, 13)
    arrived(nb, lf_r, 12)
    left_here = added(nb, lf_s[b], lf_r).astype(BF16)
    lf_c[...] = left_here

    @pl.when(b == z)
    def _():
        lf[c * nz + z] = left_here

    @pl.when(b != z)
    def _():
        put(lf_c, lf.at[c * nz + b], sends.at[14], recvs.at[14], twin)

    arrived(nb, pj, 13)
    proj = pj[...].astype(F32).reshape(QR, cols_in).astype(BF16)

    slots = rt_s.shape[0] // 4
    tall_rows = slots * rt_s.shape[1]
    for i in range(4):
        r = nt(ein[pl.ds(i * tall_rows, tall_rows), :], proj)
        rt_s[pl.ds(i * slots, slots)] = r.reshape(slots, rt_s.shape[1], QR).astype(BF16)
    to_mate(rt_s.at[pl.ds((1 - c) * nz, nz)], rt_p, 15)
    wait_bytes(rt_p, recvs.at[15])
    rt_z[...] = (rt_s[pl.ds(c * nz, nz)].astype(F32) + rt_p[...].astype(F32)).astype(BF16)
    scatter(nz, zdev, z, rt_z, 0, rt_r, 16)

    @pl.when(b != z)
    def _():
        wait_bytes(lf_c, recvs.at[14])
        wait_bytes(lf_c, sends.at[14])

    spread(nz, zdev, lf, c * nz + z, 17)
    arrived(nz, rt_r, 16)
    rt[c * nz + z] = added(nz, rt_z[z], rt_r).astype(BF16)
    spread(nz, zdev, rt, c * nz + z, 18)
    arrived(nz, lf, 17)
    to_mate(lf.at[pl.ds(c * nz, nz)], lf.at[pl.ds(c * nz, nz)], 19)
    arrived(nz, rt, 18)
    to_mate(rt.at[pl.ds(c * nz, nz)], rt.at[pl.ds(c * nz, nz)], 20)

    loads[6].wait()
    loads[7].wait()
    loads[8].wait()
    wait_bytes(lf.at[pl.ds(0, nz)], recvs.at[19])
    left = lf[...].astype(F32).reshape(gr.shape[1], QR).astype(BF16)
    tk_s[:, :, QR:] = nn(gr[...], left).reshape(nb, -1, QR)
    half = act.shape[1] // 2
    tokens = act.shape[0]
    wait_bytes(rt.at[pl.ds(0, nz)], recvs.at[20])
    tok = None
    for i in range(2):
        right = rt[pl.ds(i * nz, nz)].astype(F32).reshape(half, QR).astype(BF16)
        t = nn(act[:, i * half : (i + 1) * half], right)
        tok = t if tok is None else tok + t
    tk_s[:, :, :QR] = tok.reshape(nb, -1, QR)
    scatter(nb, bdev, b, tk_s, 0, tk_r, 21)

    here = d * tokens + iota((tokens, lens.shape[1]), 0)
    length = lens[...].astype(F32)
    earlier = jnp.where(
        iota((lens.shape[1],) * 2, 0) < iota((lens.shape[1],) * 2, 1), 1.0, 0.0
    ).astype(BF16)
    start = nn(jnp.broadcast_to(length, (8, lens.shape[1])).astype(BF16), earlier)[0:1, :]
    stop = start + length
    place = here.astype(F32)
    member = jnp.where((place >= start) & (place < stop), 1.0, 0.0).astype(F32)
    pick = jnp.where(
        lax.div(iota((QR, 128), 0), RANK) == iota((QR, 128), 1), 1.0, 0.0
    ).astype(F32)

    arrived(nb, tk_r, 21)
    both = added(nb, tk_s[b], tk_r)
    sc[b] = nn(both[:, :QR] * both[:, QR:], pick, HIGHEST)
    spread(nb, bdev, sc, b, 22)
    arrived(nb, sc, 22)
    every = sc[...].reshape(tokens, 128)
    scores_o[...] = every[:, :QUERIES]
    dc_s[...] = tn(every, member, HIGHEST)[0:8, :]
    to_mate(dc_s, dc_p, 23)
    wait_bytes(dc_p, recvs.at[23])
    dc_z[...] = dc_s[...] + dc_p[...]
    for k in near_first(nz):
        put(dc_z, dc_r.at[k], sends.at[24], recvs.at[24], zdev(k))
    sent.append((dc_r.at[pl.ds(0, nz - 1)], sends.at[24]))
    arrived(nz, dc_r, 24)
    docs = added(nz, dc_z[...], dc_r)
    full = jnp.concatenate([docs, jnp.zeros((120, docs.shape[1]), F32)], axis=0)
    doc_o[...] = full.T[:, :QUERIES]
    for ref, sem in sent:
        wait_bytes(ref, sem)


def local(nb, nz, eig_in, eig_out, eigvals, out_factors, in_factors, test_matrix, activations, gradients, doc_lengths):
    ra, cj = eig_in.shape
    ri, ca = eig_out.shape
    tokens = activations.shape[0]
    docs = doc_lengths.shape[0]
    nd = 2 * nz
    vm = pltpu.VMEM
    scratch = [
        vm((ra, cj), BF16),
        vm((ri, ca), BF16),
        vm((ri, cj), BF16),
        vm(out_factors.shape, BF16),
        vm(test_matrix.shape, BF16),
        vm(activations.shape, BF16),
        vm(gradients.shape, BF16),
        vm((1, docs), jnp.int32),
        vm((nd, ra // nd, QC), BF16),
        vm((QC, cj), F32),
        vm((ri, cj), F32),
        vm((QUERIES, cj, QR), BF16),
        vm((QUERIES, ri, cj), BF16),
        vm((nb, QC // nb, cj), BF16),
        vm((nb, QC // nb, cj), BF16),
        vm((nb, QC // nb, cj), BF16),
        vm((nd, ri // nd, QC), BF16),
        vm((nz, ri // nd, QC), BF16),
        vm((nz, ri // nd, QC), BF16),
        vm((nz, ri // nd, QC), BF16),
        vm((nd, ri // nd, QC), BF16),
        vm((nd, ri // nd, QR), BF16),
        vm((nz, ri // nd, QR), BF16),
        vm((nz, ri // nd, QR), BF16),
        vm((nz, ri // nd, QR), BF16),
        vm((nd, ri // nd, QR), BF16),
        vm((RANK, QR), F32),
        vm((nb, RANK, QR), F32),
        vm((nb, QR // nb, cj), BF16),
        vm((nb, QR // nb, cj), BF16),
        vm((nb, QR // nb, cj), BF16),
        vm((nb, ca // nb, QR), BF16),
        vm((nb, ca // nb, QR), BF16),
        vm((ca // nb, QR), BF16),
        vm((nd, ca // nb, QR), BF16),
        vm((nd, ra // nd, QR), BF16),
        vm((nz, ra // nd, QR), BF16),
        vm((nz, ra // nd, QR), BF16),
        vm((nz, ra // nd, QR), BF16),
        vm((nd, ra // nd, QR), BF16),
        vm((nb, tokens // nb, 2 * QR), F32),
        vm((nb, tokens // nb, 2 * QR), F32),
        vm((nb, tokens // nb, 128), F32),
        vm((8, docs), F32),
        vm((8, docs), F32),
        vm((8, docs), F32),
        vm((nz, 8, docs), F32),
        pltpu.SemaphoreType.DMA((9,)),
        pltpu.SemaphoreType.DMA(()),
        pltpu.SemaphoreType.DMA((nz,)),
        pltpu.SemaphoreType.DMA(()),
        pltpu.SemaphoreType.DMA((nz,)),
        pltpu.SemaphoreType.DMA((25,)),
        pltpu.SemaphoreType.DMA((25,)),
    ]
    return pl.pallas_call(
        functools.partial(body, nb, nz),
        out_shape=(
            jax.ShapeDtypeStruct((tokens, QUERIES), F32),
            jax.ShapeDtypeStruct((docs, QUERIES), F32),
        ),
        in_specs=[pl.BlockSpec(memory_space=pl.ANY)] * 9,
        out_specs=(pl.BlockSpec(memory_space=pltpu.VMEM), pl.BlockSpec(memory_space=pltpu.VMEM)),
        scratch_shapes=scratch,
        compiler_params=pltpu.CompilerParams(
            collective_id=0, has_side_effects=True, vmem_limit_bytes=60 * 1024 * 1024
        ),
        name="influence",
    )(
        eig_in,
        eig_out,
        eigvals,
        out_factors,
        in_factors,
        test_matrix,
        activations,
        gradients,
        doc_lengths.reshape(1, docs),
    )


def solution(mesh):
    nb = mesh.shape["basis"]
    nz = mesh.shape["docs"] // 2
    return jax.shard_map(
        functools.partial(local, nb, nz),
        mesh=mesh,
        in_specs=(
            P("basis", "docs"),
            P("basis", "docs"),
            P("basis", "docs"),
            P("docs", None),
            P(("basis", "docs"), None),
            P("docs", None),
            P("docs", "basis"),
            P("docs", "basis"),
            P(),
        ),
        out_specs=(P("docs", None), P()),
        check_vma=False,
    )
```

time: 915 us -> 170 us (0.19)
  blocking collectives: 518 us -> 0 us
  waiting for transfers between devices: 317 us -> 0 us
  Pallas kernels: 0 us -> 165 us
  matrix products: 29.2 us -> 0 us
  other arithmetic: 27.9 us -> 0 us
  between operations: 13.9 us -> 0.64 us
    psum x6 -> x0, blocking collectives: 478 us -> none  [the longest x1 126 us: local(): right_factor = lax.psum(right_part, 'docs').astype(jnp.bfloat16)]
    psum x2 -> x0, waiting for transfers between devices: 317 us -> none  [the longest x1 205 us: local(): sketch = lax.psum(sketch_part, 'docs')]
    pallas_call x0 -> x1, Pallas kernels: none -> 165 us  [local(): pl.pallas_call(functools.partial(body, nb, nz), out_shape=(jax.ShapeDtype...]
    all_gather x1 -> x0, blocking collectives: 40.4 us -> none  [local(): lax.all_gather(in_factors, 'docs', axis=0, tiled=True)]
    dot_general x11 -> x0, matrix products: 27.8 us -> none  [the longest x1 7.3 us: local(): jnp.einsum('qri,qij->qrj', range_rows, moment, precision=highest)]
    another operation x9 -> x0, other arithmetic: 24.1 us -> none  [the longest x4 12.6 us: local(): lower_factor = jnp.linalg.cholesky(gram_sum)]
  transfers between devices with their start and end apart: 3 -> 0, of which waited for: 2 -> 0; matrix products, arithmetic and copies ran while one was open for 0% -> 0% of each run, Pallas kernels for 0% -> 0%
where the time goes in v1:
time: 170 us
  Pallas kernels  165 us (97%)
  local copies, waits for them, and re-layouts  4.62 us (3%)
    pallas_call x1, Pallas kernels, local(): pl.pallas_call(functools.partial(body, nb, nz), out_shape=(jax.ShapeDtype...  165 us

profile of v1, /device:TPU:1, one launch (start us, length us, event | category | flops | bytes accessed | tf_op | source)
XLA Modules:
  0.0 169.9 jit_solution(13061550055448666485)
XLA Ops:
  0.6 1.6 copy.11.te_h
  2.3 164.7 %influence.1 = (f32[128,4]{1,0:T(8,128)}, f32[128,4]{1,0:T(8,128)}) custom-call(bf16[1792,896]{1,0:T(8,128)(2,1)} %ein_h.1, bf16[512,256]{1,0:T(8,128)(2,1)} %eout_h.1, bf16[512,896]{1,0:T(8,128)(2,1)} %lam_h.1, bf16[256,256]{1,0:T(8,128)(2,1)} %of_h.1, bf16[56,256]{1,0:T(8,128)(2,1)} %inf_h.1, bf16[896,32]{1,0:T(8,128)(2,1)} %copy.11.te_h, ...), custom_call_target="tpu_custom_call" | custom-call | tf_op jit(solution)/shard_map/influence/pallas_call | solution.py:495
  166.9 1.5 copy.12
  168.4 1.5 copy.13

commit v2 on v1

--- a/solution.py
+++ b/solution.py
@@ -42,6 +42,14 @@
         if n - k != k:
             order.append(n - k)
     return order
+
+
+def tree(n):
+    if n == 16:
+        return (6, -6, 3, -3), ((6, 2),)
+    if n == 4:
+        return (), ((0, 2),)
+    return (), ()
 
 
 def wait_bytes(ref, sem):
@@ -100,6 +108,8 @@
     rt_s,
     rt_p,
     rt_z,
+    rt_l,
+    rt_a,
     rt_r,
     rt,
     tk_s,
@@ -114,6 +124,11 @@
     a_recv,
     f_send,
     f_recv,
+    l_send,
+    l_recv,
+    j_send,
+    j_recv,
+    g_recv,
     sends,
     recvs,
 ):
@@ -125,7 +140,7 @@
     sent = []
 
     def zdev(k):
-        return {"docs": lax.rem(z + k, nz) * 2 + c}
+        return {"docs": lax.rem(z + k + nz, nz) * 2 + c}
 
     def bdev(k):
         return {"basis": lax.rem(b + k, nb)}
@@ -196,9 +211,62 @@
 
     pl.semaphore_wait(barrier, nz + nb - 1 + jnp.where(b != z, 1, 0))
 
+    jumps, extra = tree(nz)
+    near = (1, -1) if nz > 2 else (1,)
+    beyond = dict(extra)
+
+    def forward(slot, off, s, r):
+        for step in near + ((beyond[off],) if off in beyond else ()):
+            put(slot(off), slot(off), s, r(off + step), zdev(step))
+
+    def tree_gather(slot, s, r):
+        for j in jumps:
+            put(slot(0), slot(0), s, r(j), zdev(j))
+        forward(slot, 0, s, r)
+
+    def slot_in(off):
+        return xin.at[lax.rem(z - off + nz, nz) * 2 + c]
+
+    def slot_of(ref):
+        return lambda off: ref.at[c * nz + lax.rem(z - off + nz, nz)]
+
+    centers = jumps + (0,)
+
+    def leaves(parts, ref, s, r):
+        count = 0
+        for i, e in enumerate(centers):
+            steps = near + ((beyond[e],) if e in beyond else ())
+            for m, step in enumerate(steps):
+                target = lax.rem(z - e - step + 2 * nz, nz)
+                put(parts.at[target], ref.at[3 * i + m], s, r.at[i], zdev(-step))
+                count += 1
+        sent.append((parts.at[pl.ds(0, count)], s))
+
+    def roots(parts, ref, agg, got, r, js, jr):
+        total = None
+        for i, e in enumerate(centers):
+            steps = near + ((beyond[e],) if e in beyond else ())
+            wait_bytes(ref.at[pl.ds(3 * i, len(steps))], r.at[i])
+            total = parts[lax.rem(z - e + nz, nz)].astype(F32)
+            for m in range(len(steps)):
+                total = total + ref[3 * i + m].astype(F32)
+            if e != 0:
+                agg[i] = total.astype(BF16)
+                put(agg.at[i], got.at[i], js, jr, zdev(-e))
+        if len(jumps) > 0:
+            sent.append((agg.at[pl.ds(0, len(jumps))], js))
+            wait_bytes(got.at[pl.ds(0, len(jumps))], jr)
+            for i in range(len(jumps)):
+                total = total + got[i].astype(F32)
+        return total
+
+    order = list(near) + ([beyond[0]] if 0 in beyond else [])
+    for j in sorted(jumps, key=abs):
+        order.append(j)
+    for j in sorted(jumps, key=abs):
+        order += [j + e for e in near] + ([j + beyond[j]] if j in beyond else [])
     loads[0].wait()
-    for k in near_first(nz):
-        put(xin.at[d], xin.at[d], a_send, a_recv.at[k], zdev(k))
+    tree_gather(slot_in, a_send, lambda off: a_recv.at[off % nz])
     sent.append((xin.at[pl.ds(0, nz - 1)], a_send))
     put(xin.at[d], xin.at[d], f_send, f_recv.at[0], mate)
 
@@ -211,19 +279,24 @@
     loads[4].wait()
     wgt[...] = 1.0 / (lam[...].astype(F32) + DAMPING)
     loads[5].wait()
-    wide = jnp.concatenate([te[...].astype(F32)] * QUERIES, axis=1)
+    wide = jnp.concatenate([te[...].astype(F32)] * QUERIES, axis=0).T
     for q in range(QUERIES):
         tsel[q] = jnp.where(lax.div(iota(wide.shape, 1), RANK) == q, wide, 0.0).astype(BF16)
 
     wait_bytes(po_p, recvs.at[0])
     po_z[...] = (po_s[pl.ds(c * nz, nz)].astype(F32) + po_p[...].astype(F32)).astype(BF16)
 
-    for k in near_first(nz):
-        origin = lax.rem(z - k + nz, nz) * 2 + c
-        pltpu.make_async_copy(xin.at[origin], xin.at[origin], a_recv.at[k]).wait()
-        put(xin.at[origin], xin.at[origin], f_send, f_recv.at[k], mate)
+    scatter(nz, zdev, z, po_z, 0, po_r, 1)
+
+    for off in order:
+        pltpu.make_async_copy(slot_in(off), slot_in(off), a_recv.at[off % nz]).wait()
+        if off in jumps:
+            forward(slot_in, off, a_send, lambda o: a_recv.at[o % nz])
+        put(slot_in(off), slot_in(off), f_send, f_recv.at[off % nz], mate)
     sent.append((xin.at[pl.ds(0, nz)], f_send))
-    scatter(nz, zdev, z, po_z, 0, po_r, 1)
+    arrived(nz, po_r, 1)
+    ro[c * nz + z] = added(nz, po_z[z], po_r).astype(BF16)
+    spread(nz, zdev, ro, c * nz + z, 3)
     for k in range(nz):
         other = lax.rem(z - k + nz, nz) * 2 + 1 - c
         pltpu.make_async_copy(xin.at[other], xin.at[other], f_recv.at[k]).wait()
@@ -243,10 +316,6 @@
             pin_s[...] = t.astype(BF16).reshape(pin_s.shape)
     scatter(nb, bdev, b, pin_s, 0, pin_r, 2)
 
-    arrived(nz, po_r, 1)
-    ro[c * nz + z] = added(nz, po_z[z], po_r).astype(BF16)
-    spread(nz, zdev, ro, c * nz + z, 3)
-
     arrived(nb, pin_r, 2)
     rin[b] = added(nb, pin_s[b], pin_r).astype(BF16)
     spread(nb, bdev, rin, b, 4)
@@ -259,21 +328,27 @@
     rows_out = eout.shape[0]
     cols_in = ein.shape[1]
     rotin = rin[...].reshape(QC, cols_in)
-    rotout = ro[...].reshape(rows_out, QC)
     step = 128
     per = sk_s.shape[1]
-    for i in range(rows_out // step):
-        block = rotout[i * step : (i + 1) * step, :]
-        lane = lax.div(iota(block.shape, 1), LQ)
-        total = None
-        for q in range(QUERIES):
-            only = jnp.where(lane == q, block.astype(F32), 0.0).astype(BF16)
-            m = (nn(only, rotin) * wgt[pl.ds(i * step, step), :]).astype(BF16)
-            mom[q, pl.ds(i * step, step), :] = m
-            t = nn(m, tsel[q])
-            total = t if total is None else total + t
-        sk_s[pl.ds(i * step // per, step // per)] = total.astype(BF16).reshape(step // per, per, QR)
-    to_mate(sk_s.at[pl.ds((1 - c) * nz, nz)], sk_p, 6)
+    per_block = step // per
+    blocks = nz // per_block
+    for h in range(2):
+        side = 1 - c if h == 0 else c
+        for i in range(blocks):
+            slot = side * nz + i * per_block
+            at = pl.multiple_of(slot * per, step)
+            block = ro[pl.ds(slot, per_block)].reshape(step, QC).astype(F32)
+            lane = lax.div(iota(block.shape, 1), LQ)
+            total = None
+            for q in range(QUERIES):
+                only = jnp.where(lane == q, block, 0.0).astype(BF16)
+                m = (nn(only, rotin) * wgt[pl.ds(at, step), :]).astype(BF16)
+                mom[q, pl.ds(at, step), :] = m
+                t = nn(m, tsel[q])
+                total = t if total is None else total + t
+            sk_s[pl.ds(slot, per_block)] = total.astype(BF16).reshape(per_block, per, QR)
+        if h == 0:
+            to_mate(sk_s.at[pl.ds((1 - c) * nz, nz)], sk_p, 6)
     wait_bytes(sk_p, recvs.at[6])
     sk_z[...] = (sk_s[pl.ds(c * nz, nz)].astype(F32) + sk_p[...].astype(F32)).astype(BF16)
     scatter(nz, zdev, z, sk_z, 0, sk_r, 7)
@@ -353,15 +428,18 @@
     arrived(nb, pj, 13)
     proj = pj[...].astype(F32).reshape(QR, cols_in).astype(BF16)
 
-    slots = rt_s.shape[0] // 4
+    slots = nz // 2
     tall_rows = slots * rt_s.shape[1]
-    for i in range(4):
-        r = nt(ein[pl.ds(i * tall_rows, tall_rows), :], proj)
-        rt_s[pl.ds(i * slots, slots)] = r.reshape(slots, rt_s.shape[1], QR).astype(BF16)
-    to_mate(rt_s.at[pl.ds((1 - c) * nz, nz)], rt_p, 15)
+    for h in range(4):
+        slot = (1 - c if h < 2 else c) * nz + (h % 2) * slots
+        at = pl.multiple_of(slot * rt_s.shape[1], tall_rows)
+        r = nt(ein[pl.ds(at, tall_rows), :], proj)
+        rt_s[pl.ds(slot, slots)] = r.reshape(slots, rt_s.shape[1], QR).astype(BF16)
+        if h == 1:
+            to_mate(rt_s.at[pl.ds((1 - c) * nz, nz)], rt_p, 15)
     wait_bytes(rt_p, recvs.at[15])
     rt_z[...] = (rt_s[pl.ds(c * nz, nz)].astype(F32) + rt_p[...].astype(F32)).astype(BF16)
-    scatter(nz, zdev, z, rt_z, 0, rt_r, 16)
+    leaves(rt_z, rt_l, l_send, l_recv)
 
     @pl.when(b != z)
     def _():
@@ -369,12 +447,16 @@
         wait_bytes(lf_c, sends.at[14])
 
     spread(nz, zdev, lf, c * nz + z, 17)
-    arrived(nz, rt_r, 16)
-    rt[c * nz + z] = added(nz, rt_z[z], rt_r).astype(BF16)
-    spread(nz, zdev, rt, c * nz + z, 18)
+    rt[c * nz + z] = roots(rt_z, rt_l, rt_a, rt_r, l_recv, j_send, j_recv).astype(BF16)
+    slot_rt = slot_of(rt)
+    tree_gather(slot_rt, sends.at[18], lambda off: g_recv.at[jumps.index(off)] if off in jumps else recvs.at[18])
     arrived(nz, lf, 17)
     to_mate(lf.at[pl.ds(c * nz, nz)], lf.at[pl.ds(c * nz, nz)], 19)
-    arrived(nz, rt, 18)
+    for j in jumps:
+        wait_bytes(slot_rt(j), g_recv.at[jumps.index(j)])
+        forward(slot_rt, j, sends.at[18], lambda off: recvs.at[18])
+    wait_bytes(rt.at[pl.ds(0, nz - 1 - len(jumps))], recvs.at[18])
+    sent.append((rt.at[pl.ds(0, nz - 1)], sends.at[18]))
     to_mate(rt.at[pl.ds(c * nz, nz)], rt.at[pl.ds(c * nz, nz)], 20)
 
     loads[6].wait()
@@ -413,8 +495,8 @@
     spread(nb, bdev, sc, b, 22)
     arrived(nb, sc, 22)
     every = sc[...].reshape(tokens, 128)
-    scores_o[...] = every[:, :QUERIES]
-    dc_s[...] = tn(every, member, HIGHEST)[0:8, :]
+    scores_o[...] = every.T[:QUERIES, :]
+    dc_s[...] = tn(every, member, HIGHEST)[0:QUERIES, :]
     to_mate(dc_s, dc_p, 23)
     wait_bytes(dc_p, recvs.at[23])
     dc_z[...] = dc_s[...] + dc_p[...]
@@ -423,8 +505,7 @@
     sent.append((dc_r.at[pl.ds(0, nz - 1)], sends.at[24]))
     arrived(nz, dc_r, 24)
     docs = added(nz, dc_z[...], dc_r)
-    full = jnp.concatenate([docs, jnp.zeros((120, docs.shape[1]), F32)], axis=0)
-    doc_o[...] = full.T[:, :QUERIES]
+    doc_o[...] = docs
     for ref, sem in sent:
         wait_bytes(ref, sem)
 
@@ -441,7 +522,7 @@
         vm((ri, ca), BF16),
         vm((ri, cj), BF16),
         vm(out_factors.shape, BF16),
-        vm(test_matrix.shape, BF16),
+        vm((RANK, cj), BF16),
         vm(activations.shape, BF16),
         vm(gradients.shape, BF16),
         vm((1, docs), jnp.int32),
@@ -475,28 +556,35 @@
         vm((nd, ra // nd, QR), BF16),
         vm((nz, ra // nd, QR), BF16),
         vm((nz, ra // nd, QR), BF16),
-        vm((nz, ra // nd, QR), BF16),
+        vm((15, ra // nd, QR), BF16),
+        vm((4, ra // nd, QR), BF16),
+        vm((4, ra // nd, QR), BF16),
         vm((nd, ra // nd, QR), BF16),
         vm((nb, tokens // nb, 2 * QR), F32),
         vm((nb, tokens // nb, 2 * QR), F32),
         vm((nb, tokens // nb, 128), F32),
-        vm((8, docs), F32),
-        vm((8, docs), F32),
-        vm((8, docs), F32),
-        vm((nz, 8, docs), F32),
+        vm((QUERIES, docs), F32),
+        vm((QUERIES, docs), F32),
+        vm((QUERIES, docs), F32),
+        vm((nz, QUERIES, docs), F32),
         pltpu.SemaphoreType.DMA((9,)),
         pltpu.SemaphoreType.DMA(()),
         pltpu.SemaphoreType.DMA((nz,)),
         pltpu.SemaphoreType.DMA(()),
         pltpu.SemaphoreType.DMA((nz,)),
+        pltpu.SemaphoreType.DMA(()),
+        pltpu.SemaphoreType.DMA((5,)),
+        pltpu.SemaphoreType.DMA(()),
+        pltpu.SemaphoreType.DMA(()),
+        pltpu.SemaphoreType.DMA((4,)),
         pltpu.SemaphoreType.DMA((25,)),
         pltpu.SemaphoreType.DMA((25,)),
     ]
-    return pl.pallas_call(
+    scores, influence = pl.pallas_call(
         functools.partial(body, nb, nz),
         out_shape=(
-            jax.ShapeDtypeStruct((tokens, QUERIES), F32),
-            jax.ShapeDtypeStruct((docs, QUERIES), F32),
+            jax.ShapeDtypeStruct((QUERIES, tokens), F32),
+            jax.ShapeDtypeStruct((QUERIES, docs), F32),
         ),
         in_specs=[pl.BlockSpec(memory_space=pl.ANY)] * 9,
         out_specs=(pl.BlockSpec(memory_space=pltpu.VMEM), pl.BlockSpec(memory_space=pltpu.VMEM)),
@@ -511,11 +599,24 @@
         eigvals,
         out_factors,
         in_factors,
-        test_matrix,
+        test_matrix.T,
         activations,
         gradients,
         doc_lengths.reshape(1, docs),
     )
+    def leave(a, b, x, y):
+        x[...] = a[...]
+        y[...] = b[...]
+
+    scores, influence = pl.pallas_call(
+        leave,
+        out_shape=(
+            jax.ShapeDtypeStruct(scores.shape, F32),
+            jax.ShapeDtypeStruct(influence.shape, F32),
+        ),
+        name="leave",
+    )(scores, influence)
+    return scores.T, influence.T
 
 
 def solution(mesh):

time: 170 us -> 144 us (0.85)
  Pallas kernels: 165 us -> 143 us
  local copies, waits for them, and re-layouts: 4.62 us -> 0 us
    pallas_call x1, Pallas kernels: 165 us -> 142 us  [local(): pl.pallas_call(functools.partial(body, nb, nz), out_shape=(jax.ShapeDtype...]
    pallas_call x2 -> x0, local copies, waits for them, and re-layouts: 2.98 us -> none  [local(): pl.pallas_call(functools.partial(body, nb, nz), out_shape=(jax.ShapeDtype...]
where the time goes in v2:
time: 144 us; the launch traced here: 143 us
  Pallas kernels  143 us (99%)
    pallas_call x1, Pallas kernels, local(): pl.pallas_call(functools.partial(body, nb, nz), out_shape=(jax.ShapeDtype...  142 us

profile of v2, /device:TPU:1, one launch (start us, length us, event | category | flops | bytes accessed | tf_op | source)
XLA Modules:
  0.0 143.5 jit_solution(1519838055537014243)
XLA Ops:
  0.6 141.6 %influence.1 = (f32[4,128]{1,0:T(4,128)}, f32[4,128]{1,0:T(4,128)}) custom-call(bf16[1792,896]{1,0:T(8,128)(2,1)} %ein_h.1, bf16[512,256]{1,0:T(8,128)(2,1)} %eout_h.1, bf16[512,896]{1,0:T(8,128)(2,1)} %lam_h.1, bf16[256,256]{1,0:T(8,128)(2,1)} %of_h.1, bf16[56,256]{1,0:T(8,128)(2,1)} %inf_h.1, bf16[32,896]{1,0:T(8,128)(2,1)} %bitcast.4, ...), custom_call_target="tpu_custom_call" | custom-call | tf_op jit(solution)/shard_map/influence/pallas_call | solution.py:583
  142.2 1.3 leave.1

commit v3 on v2

--- a/solution.py
+++ b/solution.py
@@ -35,13 +35,18 @@
     return lax.broadcasted_iota(jnp.int32, shape, axis)
 
 
-def near_first(n):
-    order = []
-    for k in range(1, n // 2 + 1):
-        order.append(k)
-        if n - k != k:
-            order.append(n - k)
-    return order
+def ring(k, n):
+    return min(k, n - k)
+
+
+def far_first(n):
+    return sorted(range(1, n), key=lambda k: -ring(k, n))
+
+
+def far_first_grid(n, side):
+    if side == 1:
+        return far_first(n)
+    return sorted(range(1, n), key=lambda k: -ring(k // side, side) - ring(k % side, side))
 
 
 def tree(n):
@@ -89,6 +94,8 @@
     po_s,
     po_p,
     po_z,
+    po_l,
+    po_a,
     po_r,
     ro,
     sk_s,
@@ -129,6 +136,11 @@
     j_send,
     j_recv,
     g_recv,
+    p_send,
+    p_recv,
+    q_send,
+    q_recv,
+    h_recv,
     sends,
     recvs,
 ):
@@ -142,8 +154,21 @@
     def zdev(k):
         return {"docs": lax.rem(z + k + nz, nz) * 2 + c}
 
+    side = 4 if nb == 16 else 2 if nb == 4 else 1
+
+    def bpeer(k):
+        if side == 1:
+            return lax.rem(b + k, nb)
+        across = lax.rem(lax.div(b, side) + k // side, side)
+        return across * side + lax.rem(lax.rem(b, side) + k % side, side)
+
+    def zpeer(k):
+        return lax.rem(z + k, nz)
+
     def bdev(k):
-        return {"basis": lax.rem(b + k, nb)}
+        return {"basis": bpeer(k)}
+
+    zfar, bfar = far_first(nz), far_first_grid(nb, side)
 
     def put(src, dst, s, r, dev):
         pltpu.make_async_remote_copy(
@@ -154,10 +179,10 @@
         put(src, dst, sends.at[ch], recvs.at[ch], mate)
         sent.append((src, sends.at[ch]))
 
-    def scatter(n, dev, me, src, base, dst, ch):
-        for k in near_first(n):
+    def scatter(n, peer, dev, far, src, dst, ch):
+        for k in far:
             put(
-                src.at[base + lax.rem(me + k, n)],
+                src.at[peer(k)],
                 dst.at[k],
                 sends.at[ch],
                 recvs.at[ch],
@@ -165,8 +190,8 @@
             )
         sent.append((dst.at[pl.ds(0, n - 1)], sends.at[ch]))
 
-    def spread(n, dev, ref, where, ch):
-        for k in near_first(n):
+    def spread(n, dev, far, ref, where, ch):
+        for k in far:
             put(ref.at[where], ref.at[where], sends.at[ch], recvs.at[ch], dev(k))
         sent.append((ref.at[pl.ds(0, n - 1)], sends.at[ch]))
 
@@ -198,9 +223,9 @@
         loads.append(cp)
 
     barrier = pltpu.get_barrier_semaphore()
-    for k in near_first(nz):
+    for k in zfar:
         pl.semaphore_signal(barrier, inc=1, device_id=zdev(k), device_id_type=MESH)
-    for k in near_first(nb):
+    for k in bfar:
         pl.semaphore_signal(barrier, inc=1, device_id=bdev(k), device_id_type=MESH)
     pl.semaphore_signal(barrier, inc=1, device_id=mate, device_id_type=MESH)
     twin = {"basis": z, "docs": b * 2 + c}
@@ -242,7 +267,7 @@
                 count += 1
         sent.append((parts.at[pl.ds(0, count)], s))
 
-    def roots(parts, ref, agg, got, r, js, jr):
+    def gather_in(parts, ref, agg, got, r, js, jr):
         total = None
         for i, e in enumerate(centers):
             steps = near + ((beyond[e],) if e in beyond else ())
@@ -255,10 +280,26 @@
                 put(agg.at[i], got.at[i], js, jr, zdev(-e))
         if len(jumps) > 0:
             sent.append((agg.at[pl.ds(0, len(jumps))], js))
+        return total
+
+    def roots(total, got, jr):
+        if len(jumps) > 0:
             wait_bytes(got.at[pl.ds(0, len(jumps))], jr)
             for i in range(len(jumps)):
                 total = total + got[i].astype(F32)
-        return total
+        return total.astype(BF16)
+
+    def relay(slot, ref, ch, rj):
+        for j in sorted(jumps, key=abs):
+            wait_bytes(slot(j), rj.at[jumps.index(j)])
+            forward(slot, j, sends.at[ch], lambda off: recvs.at[ch])
+        sent.append((ref.at[pl.ds(0, nz - 1)], sends.at[ch]))
+
+    def launch(slot, ch, rj):
+        tree_gather(slot, sends.at[ch], lambda off: rj.at[jumps.index(off)] if off in jumps else recvs.at[ch])
+
+    def landed(ref, ch):
+        wait_bytes(ref.at[pl.ds(0, nz - 1 - len(jumps))], recvs.at[ch])
 
     order = list(near) + ([beyond[0]] if 0 in beyond else [])
     for j in sorted(jumps, key=abs):
@@ -286,17 +327,21 @@
     wait_bytes(po_p, recvs.at[0])
     po_z[...] = (po_s[pl.ds(c * nz, nz)].astype(F32) + po_p[...].astype(F32)).astype(BF16)
 
-    scatter(nz, zdev, z, po_z, 0, po_r, 1)
-
-    for off in order:
+    leaves(po_z, po_l, p_send, p_recv)
+
+    def take_in(off):
         pltpu.make_async_copy(slot_in(off), slot_in(off), a_recv.at[off % nz]).wait()
         if off in jumps:
             forward(slot_in, off, a_send, lambda o: a_recv.at[o % nz])
         put(slot_in(off), slot_in(off), f_send, f_recv.at[off % nz], mate)
+
+    split = len(order) - sum(len(near) + (j in beyond) for j in jumps)
+    for off in order[:split]:
+        take_in(off)
+    out_sum = gather_in(po_z, po_l, po_a, po_r, p_recv, q_send, q_recv)
+    for off in order[split:]:
+        take_in(off)
     sent.append((xin.at[pl.ds(0, nz)], f_send))
-    arrived(nz, po_r, 1)
-    ro[c * nz + z] = added(nz, po_z[z], po_r).astype(BF16)
-    spread(nz, zdev, ro, c * nz + z, 3)
     for k in range(nz):
         other = lax.rem(z - k + nz, nz) * 2 + 1 - c
         pltpu.make_async_copy(xin.at[other], xin.at[other], f_recv.at[k]).wait()
@@ -314,13 +359,17 @@
         else:
             t = acc[...] + t
             pin_s[...] = t.astype(BF16).reshape(pin_s.shape)
-    scatter(nb, bdev, b, pin_s, 0, pin_r, 2)
+    scatter(nb, bpeer, bdev, bfar, pin_s, pin_r, 2)
+    ro[c * nz + z] = roots(out_sum, po_r, q_recv)
+    slot_ro = slot_of(ro)
+    launch(slot_ro, 3, h_recv)
 
     arrived(nb, pin_r, 2)
     rin[b] = added(nb, pin_s[b], pin_r).astype(BF16)
-    spread(nb, bdev, rin, b, 4)
-
-    arrived(nz, ro, 3)
+    spread(nb, bdev, bfar, rin, b, 4)
+
+    relay(slot_ro, ro, 3, h_recv)
+    landed(ro, 3)
     to_mate(ro.at[pl.ds(c * nz, nz)], ro.at[pl.ds(c * nz, nz)], 5)
     wait_bytes(ro.at[pl.ds(0, nz)], recvs.at[5])
     arrived(nb, rin, 4)
@@ -333,9 +382,9 @@
     per_block = step // per
     blocks = nz // per_block
     for h in range(2):
-        side = 1 - c if h == 0 else c
+        who = 1 - c if h == 0 else c
         for i in range(blocks):
-            slot = side * nz + i * per_block
+            slot = who * nz + i * per_block
             at = pl.multiple_of(slot * per, step)
             block = ro[pl.ds(slot, per_block)].reshape(step, QC).astype(F32)
             lane = lax.div(iota(block.shape, 1), LQ)
@@ -351,10 +400,10 @@
             to_mate(sk_s.at[pl.ds((1 - c) * nz, nz)], sk_p, 6)
     wait_bytes(sk_p, recvs.at[6])
     sk_z[...] = (sk_s[pl.ds(c * nz, nz)].astype(F32) + sk_p[...].astype(F32)).astype(BF16)
-    scatter(nz, zdev, z, sk_z, 0, sk_r, 7)
+    scatter(nz, zpeer, zdev, zfar, sk_z, sk_r, 7)
     arrived(nz, sk_r, 7)
     sk[c * nz + z] = added(nz, sk_z[z], sk_r).astype(BF16)
-    spread(nz, zdev, sk, c * nz + z, 8)
+    spread(nz, zdev, zfar, sk, c * nz + z, 8)
     arrived(nz, sk, 8)
     to_mate(sk.at[pl.ds(c * nz, nz)], sk.at[pl.ds(c * nz, nz)], 9)
     wait_bytes(sk.at[pl.ds(0, nz)], recvs.at[9])
@@ -366,7 +415,7 @@
     for q in range(QUERIES):
         mine = mine + jnp.where(lane_q == q, gram[q * RANK : (q + 1) * RANK, :], 0.0)
     gm_s[...] = mine
-    for k in near_first(nb):
+    for k in bfar:
         put(gm_s, gm_r.at[k], sends.at[10], recvs.at[10], bdev(k))
     sent.append((gm_r.at[pl.ds(0, nb - 1)], sends.at[10]))
 
@@ -378,41 +427,51 @@
 
     arrived(nb, gm_r, 10)
     a0 = added(nb, mine, gm_r)
-    row = iota((RANK, QR), 0)
-    lane = iota((RANK, QR), 1)
-    in_q = lane - lane_q * RANK
+    group = 8
+    spot = iota((group, QR), 0)
+    lane_t = lax.div(iota((group, QR), 1), RANK)
+    in_q = iota((group, QR), 1) - lane_t * RANK
 
     def over_lanes(x):
-        out = jnp.zeros((RANK, QR), F32)
+        out = None
         for q in range(QUERIES):
-            s = jnp.sum(jnp.where(lane_q == q, x, 0.0), axis=1, keepdims=True)
-            out = jnp.where(lane_q == q, s, out)
+            s = jnp.sum(jnp.where(lane_t == q, x, 0.0), axis=1, keepdims=True)
+            out = jnp.broadcast_to(s, x.shape) if out is None else jnp.where(lane_t == q, s, out)
         return out
 
-    def eliminate(k, carry):
-        a, e = carry
-        col = over_lanes(jnp.where(in_q == k, a, 0.0))
-        at = row == k
-        pivot = jnp.sum(jnp.where(at, col, 0.0), axis=0, keepdims=True)
-        row_a = jnp.sum(jnp.where(at, a, 0.0), axis=0, keepdims=True)
-        row_e = jnp.sum(jnp.where(at, e, 0.0), axis=0, keepdims=True)
-        f = jnp.where(row > k, col / pivot, 0.0)
-        return a - f * row_a, e - f * row_e
-
-    e0 = jnp.where(in_q == row, 1.0, 0.0).astype(F32)
-    a1, e1 = lax.fori_loop(0, RANK, eliminate, (a0, e0))
-    inv = e1 / jnp.sqrt(over_lanes(jnp.where(in_q == row, a1, 0.0)))
+    tiles = RANK // group
+    a = [a0[t * group : (t + 1) * group, :] for t in range(tiles)]
+    e = [jnp.where(in_q == spot + t * group, 1.0, 0.0).astype(F32) for t in range(tiles)]
+    for k in range(RANK):
+        first, at = k // group, k % group
+        col = [over_lanes(jnp.where(in_q == k, a[t], 0.0)) for t in range(first, tiles)]
+        pivot = 1.0 / col[0][at : at + 1, :]
+        row_a = a[first][at : at + 1, :] * pivot
+        row_e = e[first][at : at + 1, :] * pivot
+        for t in range(first, tiles):
+            f = col[t - first]
+            if t == first:
+                f = jnp.where(spot > at, f, 0.0)
+            a[t] = a[t] - f * row_a
+            e[t] = e[t] - f * row_e
+    inv = jnp.concatenate(
+        [
+            e[t] / jnp.sqrt(over_lanes(jnp.where(in_q == spot + t * group, a[t], 0.0)))
+            for t in range(tiles)
+        ],
+        axis=0,
+    )
     tall = jnp.concatenate([inv] * QUERIES, axis=0)
     same = lax.div(iota((QR, QR), 0), RANK) == lax.div(iota((QR, QR), 1), RANK)
     solve = jnp.where(same, tall, 0.0)
 
     pj_s[...] = nn(solve, acc[pl.ds(0, QR), :], HIGHEST).reshape(pj_s.shape).astype(BF16)
-    scatter(nb, bdev, b, pj_s, 0, pj_r, 11)
+    scatter(nb, bpeer, bdev, bfar, pj_s, pj_r, 11)
     lf_s[...] = nn(solve, left_raw, HIGHEST).T.reshape(lf_s.shape).astype(BF16)
-    scatter(nb, bdev, b, lf_s, 0, lf_r, 12)
+    scatter(nb, bpeer, bdev, bfar, lf_s, lf_r, 12)
     arrived(nb, pj_r, 11)
     pj[b] = added(nb, pj_s[b], pj_r).astype(BF16)
-    spread(nb, bdev, pj, b, 13)
+    spread(nb, bdev, bfar, pj, b, 13)
     arrived(nb, lf_r, 12)
     left_here = added(nb, lf_s[b], lf_r).astype(BF16)
     lf_c[...] = left_here
@@ -446,17 +505,15 @@
         wait_bytes(lf_c, recvs.at[14])
         wait_bytes(lf_c, sends.at[14])
 
-    spread(nz, zdev, lf, c * nz + z, 17)
-    rt[c * nz + z] = roots(rt_z, rt_l, rt_a, rt_r, l_recv, j_send, j_recv).astype(BF16)
+    spread(nz, zdev, zfar, lf, c * nz + z, 17)
+    own = gather_in(rt_z, rt_l, rt_a, rt_r, l_recv, j_send, j_recv)
+    rt[c * nz + z] = roots(own, rt_r, j_recv)
     slot_rt = slot_of(rt)
-    tree_gather(slot_rt, sends.at[18], lambda off: g_recv.at[jumps.index(off)] if off in jumps else recvs.at[18])
+    launch(slot_rt, 18, g_recv)
     arrived(nz, lf, 17)
     to_mate(lf.at[pl.ds(c * nz, nz)], lf.at[pl.ds(c * nz, nz)], 19)
-    for j in jumps:
-        wait_bytes(slot_rt(j), g_recv.at[jumps.index(j)])
-        forward(slot_rt, j, sends.at[18], lambda off: recvs.at[18])
-    wait_bytes(rt.at[pl.ds(0, nz - 1 - len(jumps))], recvs.at[18])
-    sent.append((rt.at[pl.ds(0, nz - 1)], sends.at[18]))
+    relay(slot_rt, rt, 18, g_recv)
+    landed(rt, 18)
     to_mate(rt.at[pl.ds(c * nz, nz)], rt.at[pl.ds(c * nz, nz)], 20)
 
     loads[6].wait()
@@ -474,7 +531,7 @@
         t = nn(act[:, i * half : (i + 1) * half], right)
         tok = t if tok is None else tok + t
     tk_s[:, :, :QR] = tok.reshape(nb, -1, QR)
-    scatter(nb, bdev, b, tk_s, 0, tk_r, 21)
+    scatter(nb, bpeer, bdev, bfar, tk_s, tk_r, 21)
 
     here = d * tokens + iota((tokens, lens.shape[1]), 0)
     length = lens[...].astype(F32)
@@ -492,7 +549,7 @@
     arrived(nb, tk_r, 21)
     both = added(nb, tk_s[b], tk_r)
     sc[b] = nn(both[:, :QR] * both[:, QR:], pick, HIGHEST)
-    spread(nb, bdev, sc, b, 22)
+    spread(nb, bdev, bfar, sc, b, 22)
     arrived(nb, sc, 22)
     every = sc[...].reshape(tokens, 128)
     scores_o[...] = every.T[:QUERIES, :]
@@ -500,7 +557,7 @@
     to_mate(dc_s, dc_p, 23)
     wait_bytes(dc_p, recvs.at[23])
     dc_z[...] = dc_s[...] + dc_p[...]
-    for k in near_first(nz):
+    for k in zfar:
         put(dc_z, dc_r.at[k], sends.at[24], recvs.at[24], zdev(k))
     sent.append((dc_r.at[pl.ds(0, nz - 1)], sends.at[24]))
     arrived(nz, dc_r, 24)
@@ -537,7 +594,9 @@
         vm((nd, ri // nd, QC), BF16),
         vm((nz, ri // nd, QC), BF16),
         vm((nz, ri // nd, QC), BF16),
-        vm((nz, ri // nd, QC), BF16),
+        vm((15, ri // nd, QC), BF16),
+        vm((4, ri // nd, QC), BF16),
+        vm((4, ri // nd, QC), BF16),
         vm((nd, ri // nd, QC), BF16),
         vm((nd, ri // nd, QR), BF16),
         vm((nz, ri // nd, QR), BF16),
@@ -577,6 +636,11 @@
         pltpu.SemaphoreType.DMA(()),
         pltpu.SemaphoreType.DMA(()),
         pltpu.SemaphoreType.DMA((4,)),
+        pltpu.SemaphoreType.DMA(()),
+        pltpu.SemaphoreType.DMA((5,)),
+        pltpu.SemaphoreType.DMA(()),
+        pltpu.SemaphoreType.DMA(()),
+        pltpu.SemaphoreType.DMA((4,)),
         pltpu.SemaphoreType.DMA((25,)),
         pltpu.SemaphoreType.DMA((25,)),
     ]

time: 144 us -> 134 us (0.931)
  Pallas kernels: 143 us -> 133 us
    pallas_call x1, Pallas kernels: 142 us -> 132 us  [local(): pl.pallas_call(functools.partial(body, nb, nz), out_shape=(jax.ShapeDtype...]
where the time goes in v3:
time: 134 us
  Pallas kernels  133 us (99%)
    pallas_call x1, Pallas kernels, local(): pl.pallas_call(functools.partial(body, nb, nz), out_shape=(jax.ShapeDtype...  132 us

profile of v3, /device:TPU:1, one launch (start us, length us, event | category | flops | bytes accessed | tf_op | source)
XLA Modules:
  0.0 134.0 jit_solution(14115294433768758944)
XLA Ops:
  0.6 132.1 %influence.1 = (f32[4,128]{1,0:T(4,128)}, f32[4,128]{1,0:T(4,128)}) custom-call(bf16[1792,896]{1,0:T(8,128)(2,1)} %ein_h.1, bf16[512,256]{1,0:T(8,128)(2,1)} %eout_h.1, bf16[512,896]{1,0:T(8,128)(2,1)} %lam_h.1, bf16[256,256]{1,0:T(8,128)(2,1)} %of_h.1, bf16[56,256]{1,0:T(8,128)(2,1)} %inf_h.1, bf16[32,896]{1,0:T(8,128)(2,1)} %bitcast.4, ...), custom_call_target="tpu_custom_call" | custom-call | tf_op jit(solution)/shard_map/influence/pallas_call | solution.py:647
  132.7 1.3 leave.1

commit v4 on v3

--- a/solution.py
+++ b/solution.py
@@ -12,6 +12,7 @@
 RANK = 32
 QR = QUERIES * RANK
 QC = QUERIES * LQ
+HC = QC // 2
 DAMPING = 0.1
 MESH = pl.DeviceIdType.MESH
 HIGHEST = lax.Precision.HIGHEST
@@ -207,7 +208,7 @@
     loads = []
     for i, (src, dst) in enumerate(
         (
-            (inf_h, xin.at[d]),
+            (inf_h.at[:, pl.ds(0, HC)], xin.at[0, d]),
             (eout_h, eout),
             (of_h, outf),
             (ein_h, ein),
@@ -216,6 +217,7 @@
             (act_h, act),
             (gr_h, gr),
             (len_h, lens),
+            (inf_h.at[:, pl.ds(HC, HC)], xin.at[1, d]),
         )
     ):
         cp = pltpu.make_async_copy(src, dst, in_sem.at[i])
@@ -234,6 +236,19 @@
     def _():
         pl.semaphore_signal(barrier, inc=1, device_id=twin, device_id_type=MESH)
 
+
+    loads[1].wait()
+    loads[2].wait()
+    part = nn(eout[...], outf[...])
+    po_s[...] = part.reshape(po_s.shape)
+
+    loads[4].wait()
+    wgt[...] = 1.0 / (lam[...].astype(F32) + DAMPING)
+    loads[5].wait()
+    wide = jnp.concatenate([te[...].astype(F32)] * QUERIES, axis=0).T
+    for q in range(QUERIES):
+        tsel[q] = jnp.where(lax.div(iota(wide.shape, 1), RANK) == q, wide, 0.0).astype(BF16)
+
     pl.semaphore_wait(barrier, nz + nb - 1 + jnp.where(b != z, 1, 0))
 
     jumps, extra = tree(nz)
@@ -249,8 +264,8 @@
             put(slot(0), slot(0), s, r(j), zdev(j))
         forward(slot, 0, s, r)
 
-    def slot_in(off):
-        return xin.at[lax.rem(z - off + nz, nz) * 2 + c]
+    def slot_in(h):
+        return lambda off: xin.at[h, lax.rem(z - off + nz, nz) * 2 + c]
 
     def slot_of(ref):
         return lambda off: ref.at[c * nz + lax.rem(z - off + nz, nz)]
@@ -306,100 +321,102 @@
         order.append(j)
     for j in sorted(jumps, key=abs):
         order += [j + e for e in near] + ([j + beyond[j]] if j in beyond else [])
-    loads[0].wait()
-    tree_gather(slot_in, a_send, lambda off: a_recv.at[off % nz])
-    sent.append((xin.at[pl.ds(0, nz - 1)], a_send))
-    put(xin.at[d], xin.at[d], f_send, f_recv.at[0], mate)
-
-    loads[1].wait()
-    loads[2].wait()
-    part = nn(eout[...], outf[...])
-    po_s[...] = part.astype(BF16).reshape(po_s.shape)
+    for h in range(2):
+        loads[9 * h].wait()
+        tree_gather(slot_in(h), a_send.at[h], lambda off: a_recv.at[h, off % nz])
+        sent.append((xin.at[h, pl.ds(0, nz - 1)], a_send.at[h]))
+        put(xin.at[h, d], xin.at[h, d], f_send.at[h], f_recv.at[h, 0], mate)
+
     to_mate(po_s.at[pl.ds((1 - c) * nz, nz)], po_p, 0)
-
-    loads[4].wait()
-    wgt[...] = 1.0 / (lam[...].astype(F32) + DAMPING)
-    loads[5].wait()
-    wide = jnp.concatenate([te[...].astype(F32)] * QUERIES, axis=0).T
-    for q in range(QUERIES):
-        tsel[q] = jnp.where(lax.div(iota(wide.shape, 1), RANK) == q, wide, 0.0).astype(BF16)
-
     wait_bytes(po_p, recvs.at[0])
-    po_z[...] = (po_s[pl.ds(c * nz, nz)].astype(F32) + po_p[...].astype(F32)).astype(BF16)
+    po_z[...] = (po_s[pl.ds(c * nz, nz)] + po_p[...]).astype(BF16)
 
     leaves(po_z, po_l, p_send, p_recv)
 
-    def take_in(off):
-        pltpu.make_async_copy(slot_in(off), slot_in(off), a_recv.at[off % nz]).wait()
-        if off in jumps:
-            forward(slot_in, off, a_send, lambda o: a_recv.at[o % nz])
-        put(slot_in(off), slot_in(off), f_send, f_recv.at[off % nz], mate)
+    def take_in(h, offs):
+        slot = slot_in(h)
+        for off in offs:
+            pltpu.make_async_copy(slot(off), slot(off), a_recv.at[h, off % nz]).wait()
+            if off in jumps:
+                forward(slot, off, a_send.at[h], lambda o: a_recv.at[h, o % nz])
+            put(slot(off), slot(off), f_send.at[h], f_recv.at[h, off % nz], mate)
+
+    pieces = xin.shape[1] // 4
+    rows = pieces * xin.shape[2]
+
+    def input_rows(h):
+        sent.append((xin.at[h, pl.ds(0, nz)], f_send.at[h]))
+        for k in range(nz):
+            other = lax.rem(z - k + nz, nz) * 2 + 1 - c
+            pltpu.make_async_copy(xin.at[h, other], xin.at[h, other], f_recv.at[h, k]).wait()
+        for i in range(4):
+            x = xin[h, pl.ds(i * pieces, pieces)].astype(F32).reshape(rows, HC).astype(BF16)
+            t = tn(x, ein[pl.ds(i * rows, rows), :])
+            if i == 0:
+                acc[pl.ds(h * HC, HC), :] = t
+            elif i < 3:
+                acc[pl.ds(h * HC, HC), :] += t
+            else:
+                t = acc[pl.ds(h * HC, HC), :] + t
+                pin_s[h] = t.reshape(pin_s.shape[1:]).astype(BF16)
+        scatter(nb, bpeer, bdev, bfar, pin_s.at[h], pin_r.at[h], (2, 1)[h])
 
     split = len(order) - sum(len(near) + (j in beyond) for j in jumps)
-    for off in order[:split]:
-        take_in(off)
+    take_in(0, order[:split])
     out_sum = gather_in(po_z, po_l, po_a, po_r, p_recv, q_send, q_recv)
-    for off in order[split:]:
-        take_in(off)
-    sent.append((xin.at[pl.ds(0, nz)], f_send))
-    for k in range(nz):
-        other = lax.rem(z - k + nz, nz) * 2 + 1 - c
-        pltpu.make_async_copy(xin.at[other], xin.at[other], f_recv.at[k]).wait()
-
+    take_in(1, order[:split])
+    take_in(0, order[split:])
     loads[3].wait()
-    pieces = xin.shape[0] // 4
-    rows = pieces * xin.shape[1]
-    for i in range(4):
-        x = xin[pl.ds(i * pieces, pieces)].astype(F32).reshape(rows, QC).astype(BF16)
-        t = tn(x, ein[pl.ds(i * rows, rows), :])
-        if i == 0:
-            acc[...] = t
-        elif i < 3:
-            acc[...] += t
-        else:
-            t = acc[...] + t
-            pin_s[...] = t.astype(BF16).reshape(pin_s.shape)
-    scatter(nb, bpeer, bdev, bfar, pin_s, pin_r, 2)
+    input_rows(0)
+    take_in(1, order[split:])
+    input_rows(1)
     ro[c * nz + z] = roots(out_sum, po_r, q_recv)
     slot_ro = slot_of(ro)
     launch(slot_ro, 3, h_recv)
 
-    arrived(nb, pin_r, 2)
-    rin[b] = added(nb, pin_s[b], pin_r).astype(BF16)
-    spread(nb, bdev, bfar, rin, b, 4)
+    for h in range(2):
+        arrived(nb, pin_r.at[h], (2, 1)[h])
+        rin[h, b] = added(nb, pin_s[h, b], pin_r.at[h]).astype(BF16)
+        spread(nb, bdev, bfar, rin.at[h], b, (4, 25)[h])
 
     relay(slot_ro, ro, 3, h_recv)
     landed(ro, 3)
     to_mate(ro.at[pl.ds(c * nz, nz)], ro.at[pl.ds(c * nz, nz)], 5)
     wait_bytes(ro.at[pl.ds(0, nz)], recvs.at[5])
-    arrived(nb, rin, 4)
 
     rows_out = eout.shape[0]
     cols_in = ein.shape[1]
-    rotin = rin[...].reshape(QC, cols_in)
     step = 128
     per = sk_s.shape[1]
     per_block = step // per
     blocks = nz // per_block
     for h in range(2):
-        who = 1 - c if h == 0 else c
-        for i in range(blocks):
-            slot = who * nz + i * per_block
-            at = pl.multiple_of(slot * per, step)
-            block = ro[pl.ds(slot, per_block)].reshape(step, QC).astype(F32)
-            lane = lax.div(iota(block.shape, 1), LQ)
-            total = None
-            for q in range(QUERIES):
-                only = jnp.where(lane == q, block, 0.0).astype(BF16)
-                m = (nn(only, rotin) * wgt[pl.ds(at, step), :]).astype(BF16)
-                mom[q, pl.ds(at, step), :] = m
-                t = nn(m, tsel[q])
-                total = t if total is None else total + t
-            sk_s[pl.ds(slot, per_block)] = total.astype(BF16).reshape(per_block, per, QR)
-        if h == 0:
-            to_mate(sk_s.at[pl.ds((1 - c) * nz, nz)], sk_p, 6)
+        arrived(nb, rin.at[h], (4, 25)[h])
+        rotin = rin[h].astype(F32).reshape(HC, cols_in).astype(BF16)
+        for g in range(2):
+            who = 1 - c if g == 0 else c
+            for i in range(blocks):
+                slot = who * nz + i * per_block
+                at = pl.multiple_of(slot * per, step)
+                block = ro[pl.ds(slot, per_block)].reshape(step, QC).astype(F32)
+                block = block[:, h * HC : (h + 1) * HC]
+                lane = lax.div(iota(block.shape, 1), LQ)
+                total = None
+                for q in range(QUERIES // 2):
+                    only = jnp.where(lane == q, block, 0.0).astype(BF16)
+                    m = (nn(only, rotin) * wgt[pl.ds(at, step), :]).astype(BF16)
+                    mom[2 * h + q, pl.ds(at, step), :] = m
+                    t = nn(m, tsel[2 * h + q])
+                    total = t if total is None else total + t
+                total = total.reshape(per_block, per, QR)
+                if h == 0:
+                    sk_s[pl.ds(slot, per_block)] = total
+                else:
+                    sk_s[pl.ds(slot, per_block)] += total
+            if h == 1 and g == 0:
+                to_mate(sk_s.at[pl.ds((1 - c) * nz, nz)], sk_p, 6)
     wait_bytes(sk_p, recvs.at[6])
-    sk_z[...] = (sk_s[pl.ds(c * nz, nz)].astype(F32) + sk_p[...].astype(F32)).astype(BF16)
+    sk_z[...] = (sk_s[pl.ds(c * nz, nz)] + sk_p[...]).astype(BF16)
     scatter(nz, zpeer, zdev, zfar, sk_z, sk_r, 7)
     arrived(nz, sk_r, 7)
     sk[c * nz + z] = added(nz, sk_z[z], sk_r).astype(BF16)
@@ -493,11 +510,11 @@
         slot = (1 - c if h < 2 else c) * nz + (h % 2) * slots
         at = pl.multiple_of(slot * rt_s.shape[1], tall_rows)
         r = nt(ein[pl.ds(at, tall_rows), :], proj)
-        rt_s[pl.ds(slot, slots)] = r.reshape(slots, rt_s.shape[1], QR).astype(BF16)
+        rt_s[pl.ds(slot, slots)] = r.reshape(slots, rt_s.shape[1], QR)
         if h == 1:
             to_mate(rt_s.at[pl.ds((1 - c) * nz, nz)], rt_p, 15)
     wait_bytes(rt_p, recvs.at[15])
-    rt_z[...] = (rt_s[pl.ds(c * nz, nz)].astype(F32) + rt_p[...].astype(F32)).astype(BF16)
+    rt_z[...] = (rt_s[pl.ds(c * nz, nz)] + rt_p[...]).astype(BF16)
     leaves(rt_z, rt_l, l_send, l_recv)
 
     @pl.when(b != z)
@@ -583,23 +600,23 @@
         vm(activations.shape, BF16),
         vm(gradients.shape, BF16),
         vm((1, docs), jnp.int32),
-        vm((nd, ra // nd, QC), BF16),
+        vm((2, nd, ra // nd, HC), BF16),
         vm((QC, cj), F32),
         vm((ri, cj), F32),
         vm((QUERIES, cj, QR), BF16),
         vm((QUERIES, ri, cj), BF16),
-        vm((nb, QC // nb, cj), BF16),
-        vm((nb, QC // nb, cj), BF16),
-        vm((nb, QC // nb, cj), BF16),
-        vm((nd, ri // nd, QC), BF16),
-        vm((nz, ri // nd, QC), BF16),
+        vm((2, nb, HC // nb, cj), BF16),
+        vm((2, nb, HC // nb, cj), BF16),
+        vm((2, nb, HC // nb, cj), BF16),
+        vm((nd, ri // nd, QC), F32),
+        vm((nz, ri // nd, QC), F32),
         vm((nz, ri // nd, QC), BF16),
         vm((15, ri // nd, QC), BF16),
         vm((4, ri // nd, QC), BF16),
         vm((4, ri // nd, QC), BF16),
         vm((nd, ri // nd, QC), BF16),
-        vm((nd, ri // nd, QR), BF16),
-        vm((nz, ri // nd, QR), BF16),
+        vm((nd, ri // nd, QR), F32),
+        vm((nz, ri // nd, QR), F32),
         vm((nz, ri // nd, QR), BF16),
         vm((nz, ri // nd, QR), BF16),
         vm((nd, ri // nd, QR), BF16),
@@ -612,8 +629,8 @@
         vm((nb, ca // nb, QR), BF16),
         vm((ca // nb, QR), BF16),
         vm((nd, ca // nb, QR), BF16),
-        vm((nd, ra // nd, QR), BF16),
-        vm((nz, ra // nd, QR), BF16),
+        vm((nd, ra // nd, QR), F32),
+        vm((nz, ra // nd, QR), F32),
         vm((nz, ra // nd, QR), BF16),
         vm((15, ra // nd, QR), BF16),
         vm((4, ra // nd, QR), BF16),
@@ -626,11 +643,11 @@
         vm((QUERIES, docs), F32),
         vm((QUERIES, docs), F32),
         vm((nz, QUERIES, docs), F32),
-        pltpu.SemaphoreType.DMA((9,)),
-        pltpu.SemaphoreType.DMA(()),
-        pltpu.SemaphoreType.DMA((nz,)),
-        pltpu.SemaphoreType.DMA(()),
-        pltpu.SemaphoreType.DMA((nz,)),
+        pltpu.SemaphoreType.DMA((10,)),
+        pltpu.SemaphoreType.DMA((2,)),
+        pltpu.SemaphoreType.DMA((2, nz)),
+        pltpu.SemaphoreType.DMA((2,)),
+        pltpu.SemaphoreType.DMA((2, nz)),
         pltpu.SemaphoreType.DMA(()),
         pltpu.SemaphoreType.DMA((5,)),
         pltpu.SemaphoreType.DMA(()),
@@ -641,8 +658,8 @@
         pltpu.SemaphoreType.DMA(()),
         pltpu.SemaphoreType.DMA(()),
         pltpu.SemaphoreType.DMA((4,)),
-        pltpu.SemaphoreType.DMA((25,)),
-        pltpu.SemaphoreType.DMA((25,)),
+        pltpu.SemaphoreType.DMA((26,)),
+        pltpu.SemaphoreType.DMA((26,)),
     ]
     scores, influence = pl.pallas_call(
         functools.partial(body, nb, nz),

time: 134 us -> 130 us (0.970)
  Pallas kernels: 133 us -> 130 us
    pallas_call x1, Pallas kernels: 132 us -> 128 us  [local(): pl.pallas_call(functools.partial(body, nb, nz), out_shape=(jax.ShapeDtype...]
where the time goes in v4:
time: 130 us
  Pallas kernels  130 us (100%)
    pallas_call x1, Pallas kernels, local(): pl.pallas_call(functools.partial(body, nb, nz), out_shape=(jax.ShapeDtype...  128 us

profile of v4, /device:TPU:1, one launch (start us, length us, event | category | flops | bytes accessed | tf_op | source)
XLA Modules:
  0.0 130.3 jit_solution(15424193158813120728)
XLA Ops:
  0.6 128.4 %influence.1 = (f32[4,128]{1,0:T(4,128)}, f32[4,128]{1,0:T(4,128)}) custom-call(bf16[1792,896]{1,0:T(8,128)(2,1)} %ein_h.1, bf16[512,256]{1,0:T(8,128)(2,1)} %eout_h.1, bf16[512,896]{1,0:T(8,128)(2,1)} %lam_h.1, bf16[256,256]{1,0:T(8,128)(2,1)} %of_h.1, bf16[56,256]{1,0:T(8,128)(2,1)} %inf_h.1, bf16[32,896]{1,0:T(8,128)(2,1)} %bitcast.4, ...), custom_call_target="tpu_custom_call" | custom-call | tf_op jit(solution)/shard_map/influence/pallas_call | solution.py:664
  129.1 1.3 leave.1

commit v5 on v4

--- a/solution.py
+++ b/solution.py
@@ -106,9 +106,12 @@
     sk,
     gm_s,
     gm_r,
-    pj_s,
-    pj_r,
-    pj,
+    pj_s0,
+    pj_s1,
+    pj_r0,
+    pj_r1,
+    pj0,
+    pj1,
     lf_s,
     lf_r,
     lf_c,
@@ -142,6 +145,7 @@
     q_send,
     q_recv,
     h_recv,
+    k_recv,
     sends,
     recvs,
 ):
@@ -225,17 +229,13 @@
         loads.append(cp)
 
     barrier = pltpu.get_barrier_semaphore()
-    for k in zfar:
+    greet = (6, 10, 3, 13, 2, 14, 1, 15) if nz == 16 else zfar
+    for k in greet:
         pl.semaphore_signal(barrier, inc=1, device_id=zdev(k), device_id_type=MESH)
     for k in bfar:
         pl.semaphore_signal(barrier, inc=1, device_id=bdev(k), device_id_type=MESH)
     pl.semaphore_signal(barrier, inc=1, device_id=mate, device_id_type=MESH)
     twin = {"basis": z, "docs": b * 2 + c}
-
-    @pl.when(b != z)
-    def _():
-        pl.semaphore_signal(barrier, inc=1, device_id=twin, device_id_type=MESH)
-
 
     loads[1].wait()
     loads[2].wait()
@@ -249,7 +249,7 @@
     for q in range(QUERIES):
         tsel[q] = jnp.where(lax.div(iota(wide.shape, 1), RANK) == q, wide, 0.0).astype(BF16)
 
-    pl.semaphore_wait(barrier, nz + nb - 1 + jnp.where(b != z, 1, 0))
+    pl.semaphore_wait(barrier, len(greet) + nb)
 
     jumps, extra = tree(nz)
     near = (1, -1) if nz > 2 else (1,)
@@ -482,13 +482,19 @@
     same = lax.div(iota((QR, QR), 0), RANK) == lax.div(iota((QR, QR), 1), RANK)
     solve = jnp.where(same, tall, 0.0)
 
-    pj_s[...] = nn(solve, acc[pl.ds(0, QR), :], HIGHEST).reshape(pj_s.shape).astype(BF16)
-    scatter(nb, bpeer, bdev, bfar, pj_s, pj_r, 11)
+    pjs, pjr, pjo = (pj_s0, pj_s1), (pj_r0, pj_r1), (pj0, pj1)
+    wide0 = pj_s0.shape[2]
+    parts_of = (pl.ds(0, wide0), pl.ds(wide0, cols_in - wide0))
+    for h in range(2):
+        ortho = nn(solve, acc[pl.ds(0, QR), parts_of[h]], HIGHEST)
+        pjs[h][...] = ortho.reshape(pjs[h].shape).astype(BF16)
+        scatter(nb, bpeer, bdev, bfar, pjs[h], pjr[h], (11, 26)[h])
     lf_s[...] = nn(solve, left_raw, HIGHEST).T.reshape(lf_s.shape).astype(BF16)
     scatter(nb, bpeer, bdev, bfar, lf_s, lf_r, 12)
-    arrived(nb, pj_r, 11)
-    pj[b] = added(nb, pj_s[b], pj_r).astype(BF16)
-    spread(nb, bdev, bfar, pj, b, 13)
+    for h in range(2):
+        arrived(nb, pjr[h], (11, 26)[h])
+        pjo[h][b] = added(nb, pjs[h][b], pjr[h]).astype(BF16)
+        spread(nb, bdev, bfar, pjo[h], b, (13, 27)[h])
     arrived(nb, lf_r, 12)
     left_here = added(nb, lf_s[b], lf_r).astype(BF16)
     lf_c[...] = left_here
@@ -501,18 +507,21 @@
     def _():
         put(lf_c, lf.at[c * nz + b], sends.at[14], recvs.at[14], twin)
 
-    arrived(nb, pj, 13)
-    proj = pj[...].astype(F32).reshape(QR, cols_in).astype(BF16)
-
     slots = nz // 2
     tall_rows = slots * rt_s.shape[1]
-    for h in range(4):
-        slot = (1 - c if h < 2 else c) * nz + (h % 2) * slots
-        at = pl.multiple_of(slot * rt_s.shape[1], tall_rows)
-        r = nt(ein[pl.ds(at, tall_rows), :], proj)
-        rt_s[pl.ds(slot, slots)] = r.reshape(slots, rt_s.shape[1], QR)
-        if h == 1:
-            to_mate(rt_s.at[pl.ds((1 - c) * nz, nz)], rt_p, 15)
+    for h in range(2):
+        arrived(nb, pjo[h], (13, 27)[h])
+        proj = pjo[h][...].astype(F32).reshape(QR, -1).astype(BF16)
+        for g in range(4):
+            slot = (1 - c if g < 2 else c) * nz + (g % 2) * slots
+            at = pl.multiple_of(slot * rt_s.shape[1], tall_rows)
+            r = nt(ein[pl.ds(at, tall_rows), parts_of[h]], proj).reshape(slots, rt_s.shape[1], QR)
+            if h == 0:
+                rt_s[pl.ds(slot, slots)] = r
+            else:
+                rt_s[pl.ds(slot, slots)] += r
+            if h == 1 and g == 1:
+                to_mate(rt_s.at[pl.ds((1 - c) * nz, nz)], rt_p, 15)
     wait_bytes(rt_p, recvs.at[15])
     rt_z[...] = (rt_s[pl.ds(c * nz, nz)] + rt_p[...]).astype(BF16)
     leaves(rt_z, rt_l, l_send, l_recv)
@@ -522,31 +531,35 @@
         wait_bytes(lf_c, recvs.at[14])
         wait_bytes(lf_c, sends.at[14])
 
-    spread(nz, zdev, zfar, lf, c * nz + z, 17)
+    slot_lf = slot_of(lf)
+    launch(slot_lf, 17, k_recv)
     own = gather_in(rt_z, rt_l, rt_a, rt_r, l_recv, j_send, j_recv)
+    relay(slot_lf, lf, 17, k_recv)
     rt[c * nz + z] = roots(own, rt_r, j_recv)
     slot_rt = slot_of(rt)
     launch(slot_rt, 18, g_recv)
-    arrived(nz, lf, 17)
+    relay(slot_rt, rt, 18, g_recv)
+    landed(lf, 17)
     to_mate(lf.at[pl.ds(c * nz, nz)], lf.at[pl.ds(c * nz, nz)], 19)
-    relay(slot_rt, rt, 18, g_recv)
     landed(rt, 18)
     to_mate(rt.at[pl.ds(c * nz, nz)], rt.at[pl.ds(c * nz, nz)], 20)
 
     loads[6].wait()
     loads[7].wait()
     loads[8].wait()
+    half = act.shape[1] // 2
+    tokens = act.shape[0]
+
+    def token_half(who):
+        right = rt[pl.ds(who * nz, nz)].astype(F32).reshape(half, QR).astype(BF16)
+        return nn(act[:, pl.ds(pl.multiple_of(who * half, half), half)], right)
+
+    tok = token_half(c)
     wait_bytes(lf.at[pl.ds(0, nz)], recvs.at[19])
     left = lf[...].astype(F32).reshape(gr.shape[1], QR).astype(BF16)
     tk_s[:, :, QR:] = nn(gr[...], left).reshape(nb, -1, QR)
-    half = act.shape[1] // 2
-    tokens = act.shape[0]
     wait_bytes(rt.at[pl.ds(0, nz)], recvs.at[20])
-    tok = None
-    for i in range(2):
-        right = rt[pl.ds(i * nz, nz)].astype(F32).reshape(half, QR).astype(BF16)
-        t = nn(act[:, i * half : (i + 1) * half], right)
-        tok = t if tok is None else tok + t
+    tok = tok + token_half(1 - c)
     tk_s[:, :, :QR] = tok.reshape(nb, -1, QR)
     scatter(nb, bpeer, bdev, bfar, tk_s, tk_r, 21)
 
@@ -591,6 +604,7 @@
     docs = doc_lengths.shape[0]
     nd = 2 * nz
     vm = pltpu.VMEM
+    wide = (cj // 2 + 127) // 128 * 128
     scratch = [
         vm((ra, cj), BF16),
         vm((ri, ca), BF16),
@@ -622,9 +636,7 @@
         vm((nd, ri // nd, QR), BF16),
         vm((RANK, QR), F32),
         vm((nb, RANK, QR), F32),
-        vm((nb, QR // nb, cj), BF16),
-        vm((nb, QR // nb, cj), BF16),
-        vm((nb, QR // nb, cj), BF16),
+        *(vm((nb, QR // nb, w), BF16) for _ in range(3) for w in (wide, cj - wide)),
         vm((nb, ca // nb, QR), BF16),
         vm((nb, ca // nb, QR), BF16),
         vm((ca // nb, QR), BF16),
@@ -658,8 +670,9 @@
         pltpu.SemaphoreType.DMA(()),
         pltpu.SemaphoreType.DMA(()),
         pltpu.SemaphoreType.DMA((4,)),
-        pltpu.SemaphoreType.DMA((26,)),
-        pltpu.SemaphoreType.DMA((26,)),
+        pltpu.SemaphoreType.DMA((4,)),
+        pltpu.SemaphoreType.DMA((28,)),
+        pltpu.SemaphoreType.DMA((28,)),
     ]
     scores, influence = pl.pallas_call(
         functools.partial(body, nb, nz),

time: 130 us -> 127 us (0.977)
  Pallas kernels: 130 us -> 127 us
    pallas_call x1, Pallas kernels: 128 us -> 125 us  [local(): pl.pallas_call(functools.partial(body, nb, nz), out_shape=(jax.ShapeDtype...]
where the time goes in v5:
time: 127 us
  Pallas kernels  127 us (100%)
    pallas_call x1, Pallas kernels, local(): pl.pallas_call(functools.partial(body, nb, nz), out_shape=(jax.ShapeDtype...  125 us

profile of v5, /device:TPU:1, one launch (start us, length us, event | category | flops | bytes accessed | tf_op | source)
XLA Modules:
  0.0 127.2 jit_solution(6015779455887524443)
XLA Ops:
  0.6 125.4 %influence.1 = (f32[4,128]{1,0:T(4,128)}, f32[4,128]{1,0:T(4,128)}) custom-call(bf16[1792,896]{1,0:T(8,128)(2,1)} %ein_h.1, bf16[512,256]{1,0:T(8,128)(2,1)} %eout_h.1, bf16[512,896]{1,0:T(8,128)(2,1)} %lam_h.1, bf16[256,256]{1,0:T(8,128)(2,1)} %of_h.1, bf16[56,256]{1,0:T(8,128)(2,1)} %inf_h.1, bf16[32,896]{1,0:T(8,128)(2,1)} %bitcast.4, ...), custom_call_target="tpu_custom_call" | custom-call | tf_op jit(solution)/shard_map/influence/pallas_call | solution.py:677
  126.0 1.3 leave.1

commit v6 on v5

--- a/solution.py
+++ b/solution.py
@@ -369,17 +369,18 @@
     loads[3].wait()
     input_rows(0)
     take_in(1, order[split:])
-    input_rows(1)
     ro[c * nz + z] = roots(out_sum, po_r, q_recv)
     slot_ro = slot_of(ro)
     launch(slot_ro, 3, h_recv)
+    input_rows(1)
 
     for h in range(2):
         arrived(nb, pin_r.at[h], (2, 1)[h])
         rin[h, b] = added(nb, pin_s[h, b], pin_r.at[h]).astype(BF16)
         spread(nb, bdev, bfar, rin.at[h], b, (4, 25)[h])
-
-    relay(slot_ro, ro, 3, h_recv)
+        if h == 0:
+            relay(slot_ro, ro, 3, h_recv)
+
     landed(ro, 3)
     to_mate(ro.at[pl.ds(c * nz, nz)], ro.at[pl.ds(c * nz, nz)], 5)
     wait_bytes(ro.at[pl.ds(0, nz)], recvs.at[5])

time: 127 us -> 126 us (level)
  Pallas kernels: 127 us -> 125 us
    pallas_call x1, Pallas kernels: 125 us -> 124 us  [local(): pl.pallas_call(functools.partial(body, nb, nz), out_shape=(jax.ShapeDtype...]
where the time goes in v6:
time: 126 us
  Pallas kernels  125 us (99%)
    pallas_call x1, Pallas kernels, local(): pl.pallas_call(functools.partial(body, nb, nz), out_shape=(jax.ShapeDtype...  124 us

profile of v6, /device:TPU:1, one launch (start us, length us, event | category | flops | bytes accessed | tf_op | source)
XLA Modules:
  0.0 125.8 jit_solution(15290932991718402880)
XLA Ops:
  0.6 123.9 %influence.1 = (f32[4,128]{1,0:T(4,128)}, f32[4,128]{1,0:T(4,128)}) custom-call(bf16[1792,896]{1,0:T(8,128)(2,1)} %ein_h.1, bf16[512,256]{1,0:T(8,128)(2,1)} %eout_h.1, bf16[512,896]{1,0:T(8,128)(2,1)} %lam_h.1, bf16[256,256]{1,0:T(8,128)(2,1)} %of_h.1, bf16[56,256]{1,0:T(8,128)(2,1)} %inf_h.1, bf16[32,896]{1,0:T(8,128)(2,1)} %bitcast.4, ...), custom_call_target="tpu_custom_call" | custom-call | tf_op jit(solution)/shard_map/influence/pallas_call | solution.py:678
  124.6 1.3 leave.1
